TPU v7x, 128 devices: a whole 4x4x4 slice. The times are simulated.
128 devices in a mesh: row: 8 (over y, x_hi), col: 16 (over x_lo, z, core).
Axes of the slice: x: 4 (x_hi: 2, x_lo: 2; x = x_hi * 2 + x_lo), y: 4, z: 4, core: 2. Of those that a mesh axis runs over, the one named last changes fastest.
Arguments:
- affinity: bfloat16 [8, 16, 32, 256, 256], P('row', 'col'), may hold values from 9e-05 to 32.4
- block_rows: int32 [8, 16, 32], P('row', 'col'), may hold values from 0 to 7, as said below
- block_cols: int32 [8, 16, 32], P('row', 'col'), may hold values from 0 to 15
- block_count: int32 [8, 16], P('row', 'col'), may hold values from 8 to 32, as said below
- labels: float32 [32768, 1024], P(('row', 'col')), may hold values from 0 to 1
- labelled: int32 [32768], P(('row', 'col')), may hold values 0 or 1
Outputs:
- scores: float32 [32768, 1024], P(('row', 'col'))
Inputs may be any that keep to these rules, and one draw needn't show every extreme that they name: Within one entry (r, c) the pairs (block_rows, block_cols) of all 32 slots are distinct, and its first 8 slots name every row block once. `block_count`: some entry has all 32 slots live.
All inputs are finite; a program needn't handle non-finite values. No bound on the sum of `labelled` on one device may be relied on, other than what follows from the above.
Results may differ from a plain program's by a relative error of at most 0.0003.
Values may be sent and summed in bfloat16 or wider, within the bound.
A program may use at most 128 MiB of HBM per device.

v0:
```python
import jax
import jax.numpy as jnp
from jax import lax
from jax.sharding import PartitionSpec as P

SWEEPS = 2


spread_weight = 0.8


def group_term(tile_stack, row_ids, col_ids, slot_live, gathered, group_id, group_width):
    first_slot = group_id * group_width
    tile_group = lax.dynamic_slice_in_dim(tile_stack, first_slot, group_width, 0)
    group_rows = lax.dynamic_slice_in_dim(row_ids, first_slot, group_width, 0)
    group_cols = lax.dynamic_slice_in_dim(col_ids, first_slot, group_width, 0)
    group_live = lax.dynamic_slice_in_dim(slot_live, first_slot, group_width, 0)
    fetched = jnp.take(gathered, group_cols, axis=0)
    product = jnp.einsum("gij,gjc->gic", tile_group, fetched, preferred_element_type=jnp.float32)
    placing = (
        (group_rows[None, :] == jnp.arange(group_width)[:, None]) & group_live[None, :]
    ).astype(jnp.float32)
    return jnp.einsum("rg,gic->ric", placing, product, precision=lax.Precision.HIGHEST)


def on_device(affinity, block_rows, block_cols, block_count, labels, labelled):
    tile_stack = affinity[0, 0]
    row_ids = block_rows[0, 0]
    col_ids = block_cols[0, 0]
    live_count = block_count[0, 0]
    row_groups = lax.axis_size("row")
    col_groups = lax.axis_size("col")
    slot_total = tile_stack.shape[0]
    tile_rows = tile_stack.shape[1]
    classes = labels.shape[1]
    slot_live = jnp.arange(slot_total) < live_count
    placing = ((row_ids[None, :] == jnp.arange(row_groups)[:, None]) & slot_live[None, :]).astype(
        jnp.float32
    )
    row_sums = jnp.sum(tile_stack, axis=2, dtype=jnp.float32)
    degree_part = jnp.dot(placing, row_sums, precision=lax.Precision.HIGHEST)
    degree = lax.psum_scatter(degree_part, "row", scatter_dimension=0, tiled=True).reshape(
        tile_rows, 1
    )
    keep_rows = labelled[:, None] == 1
    current = labels
    group_total = slot_total // row_groups
    for iteration in range(SWEEPS):
        gathered = lax.all_gather(current.astype(jnp.bfloat16), "col", axis=0, tiled=True)
        gathered = gathered.reshape(col_groups, tile_rows, classes)

        def add_group(group_id, running):
            return running + group_term(
                tile_stack, row_ids, col_ids, slot_live, gathered, group_id, row_groups
            )

        empty = jnp.zeros((row_groups, tile_rows, classes), jnp.float32)
        running = lax.fori_loop(0, group_total, add_group, empty)
        flat_terms = running.reshape(row_groups * tile_rows, classes)
        summed = lax.psum_scatter(flat_terms, "row", scatter_dimension=0, tiled=True)
        spread = spread_weight * summed / degree + (1.0 - spread_weight) * labels
        current = jnp.where(keep_rows, labels, spread)
    return current


def solution(mesh):
    placed = (
        P("row", "col", None, None, None),
        P("row", "col", None),
        P("row", "col", None),
        P("row", "col"),
        P(("row", "col"), None),
        P(("row", "col")),
    )
    return jax.shard_map(
        on_device, mesh=mesh, in_specs=placed, out_specs=P(("row", "col"), None), check_vma=False
    )
```

profile of v0, /device:TPU:0, one launch (start us, length us, event | category | flops | bytes accessed | tf_op | source)
XLA Modules:
  0.0 628.5 jit_solution(13757299641391947367)
XLA Ops:
  6.5 2.1 convert_element_type.16
  9.4 54.3 %all-gather.3.cloned.1.call-done = bf16[4096,1024]{1,0:T(8,128)(2,1)} async-done(((bf16[256,1024]{1,0:T(8,128)(2,1)}), bf16[4096,1024]{1,0:T(8,128)(2,1)}) %all-gather.3.cloned.1.call-update) | async-done | bytes 8388624 | tf_op jit(solution)/shard_map/all_gather | solution.py:49
  63.7 125.6 %while.28 = (s32[]{:T(128)}, f32[8,256,1024]{2,0,1:T(8,128)}, s32[32]{0:T(128)}, pred[32]{0:T(512)(128)(4,1)S(1)}, bf16[32,256,256]{2,1,0:T(8,128)(2,1)}, /*inde...) while((s32[]{:T(128)}, f32[8,256,1024]{2,0,1:T(8,128)}, ...), condition=%wide.region_1.3_spmd.clone, body=%wide.region_0.2_spmd.clone.sunk | while | flops 1281361024 | bytes 47191000 | solution.py:58
  63.7 0.7 compare_and_fusion.4
  64.5 6.2 gather_fusion
  70.6 7.1 %fusion.52 = f32[8,256,1024]{2,1,0:T(8,128)} fusion(bf16[8,256,1024]{2,1,0:T(8,128)(2,1)} %gather_fusion, pred[8]{0:T(512)(128)(4,1)S(1)} %get-tuple-element.420, bf16[32,256,256]{2,1,0:T(8,128)(2,1)} %get-tuple-element.456, s32[]{:T(128)S(6)} %select_n.59), kind=kOutput, calls=%fused_computation.5.clone.1 | convolution fusion | flops 1075838976 | bytes 13631500 | tf_op jit(solution)/shard_map/while/body/eval_jaxpr/gij,gjc->gic/dot_general | solution.py:19
  77.7 0.1 dynamic_slice.79
  77.8 0.1 dynamic_slice.80
  77.9 15.5 %select_add_fusion.4 = f32[8,256,1024]{2,0,1:T(8,128)} fusion(f32[8,256,1024]{2,0,1:T(8,128)} %get-tuple-element.442, pred[]{:T(512)S(6)} %compare.6, f32[8,256,1024]{2,1,0:T(8,128)} %fusion.52, s32[8]{0:T(128)S(1)} %dynamic_slice.79, pred[8]{0:T(512)(128)(4,1)S(1)} %dynamic_slice.80), kind=kOutput, calls=%fused_computation.4.clone.1 | convolution fusion | flops 205521024 | bytes 25165864 | tf_op jit(solution)/shard_map/while/body/eval_jaxpr/rg,gic->ric/dot_general | solution.py:23
  93.3 0.7 compare_and_fusion.4
  94.1 6.2 gather_fusion
  100.2 7.1 %fusion.52 = f32[8,256,1024]{2,1,0:T(8,128)} fusion(bf16[8,256,1024]{2,1,0:T(8,128)(2,1)} %gather_fusion, pred[8]{0:T(512)(128)(4,1)S(1)} %get-tuple-element.420, bf16[32,256,256]{2,1,0:T(8,128)(2,1)} %get-tuple-element.456, s32[]{:T(128)S(6)} %select_n.59), kind=kOutput, calls=%fused_computation.5.clone.1 | convolution fusion | flops 1075838976 | bytes 13631500 | tf_op jit(solution)/shard_map/while/body/eval_jaxpr/gij,gjc->gic/dot_general | solution.py:19
  107.3 0.1 dynamic_slice.79
  107.4 0.1 dynamic_slice.80
  107.5 17.9 %select_add_fusion.4 = f32[8,256,1024]{2,0,1:T(8,128)} fusion(f32[8,256,1024]{2,0,1:T(8,128)} %get-tuple-element.442, pred[]{:T(512)S(6)} %compare.6, f32[8,256,1024]{2,1,0:T(8,128)} %fusion.52, s32[8]{0:T(128)S(1)} %dynamic_slice.79, pred[8]{0:T(512)(128)(4,1)S(1)} %dynamic_slice.80), kind=kOutput, calls=%fused_computation.4.clone.1 | convolution fusion | flops 205521024 | bytes 25165864 | tf_op jit(solution)/shard_map/while/body/eval_jaxpr/rg,gic->ric/dot_general | solution.py:23
  125.3 0.7 compare_and_fusion.4
  126.1 6.2 gather_fusion
  132.2 7.1 %fusion.52 = f32[8,256,1024]{2,1,0:T(8,128)} fusion(bf16[8,256,1024]{2,1,0:T(8,128)(2,1)} %gather_fusion, pred[8]{0:T(512)(128)(4,1)S(1)} %get-tuple-element.420, bf16[32,256,256]{2,1,0:T(8,128)(2,1)} %get-tuple-element.456, s32[]{:T(128)S(6)} %select_n.59), kind=kOutput, calls=%fused_computation.5.clone.1 | convolution fusion | flops 1075838976 | bytes 13631500 | tf_op jit(solution)/shard_map/while/body/eval_jaxpr/gij,gjc->gic/dot_general | solution.py:19
  139.3 0.1 dynamic_slice.79
  139.4 0.1 dynamic_slice.80
  139.5 17.9 %select_add_fusion.4 = f32[8,256,1024]{2,0,1:T(8,128)} fusion(f32[8,256,1024]{2,0,1:T(8,128)} %get-tuple-element.442, pred[]{:T(512)S(6)} %compare.6, f32[8,256,1024]{2,1,0:T(8,128)} %fusion.52, s32[8]{0:T(128)S(1)} %dynamic_slice.79, pred[8]{0:T(512)(128)(4,1)S(1)} %dynamic_slice.80), kind=kOutput, calls=%fused_computation.4.clone.1 | convolution fusion | flops 205521024 | bytes 25165864 | tf_op jit(solution)/shard_map/while/body/eval_jaxpr/rg,gic->ric/dot_general | solution.py:23
  157.3 0.7 compare_and_fusion.4
  158.0 6.2 gather_fusion
  164.2 7.1 %fusion.52 = f32[8,256,1024]{2,1,0:T(8,128)} fusion(bf16[8,256,1024]{2,1,0:T(8,128)(2,1)} %gather_fusion, pred[8]{0:T(512)(128)(4,1)S(1)} %get-tuple-element.420, bf16[32,256,256]{2,1,0:T(8,128)(2,1)} %get-tuple-element.456, s32[]{:T(128)S(6)} %select_n.59), kind=kOutput, calls=%fused_computation.5.clone.1 | convolution fusion | flops 1075838976 | bytes 13631500 | tf_op jit(solution)/shard_map/while/body/eval_jaxpr/gij,gjc->gic/dot_general | solution.py:19
  171.3 0.1 dynamic_slice.79
  171.4 0.1 dynamic_slice.80
  171.4 17.9 %select_add_fusion.4 = f32[8,256,1024]{2,0,1:T(8,128)} fusion(f32[8,256,1024]{2,0,1:T(8,128)} %get-tuple-element.442, pred[]{:T(512)S(6)} %compare.6, f32[8,256,1024]{2,1,0:T(8,128)} %fusion.52, s32[8]{0:T(128)S(1)} %dynamic_slice.79, pred[8]{0:T(512)(128)(4,1)S(1)} %dynamic_slice.80), kind=kOutput, calls=%fused_computation.4.clone.1 | convolution fusion | flops 205521024 | bytes 25165864 | tf_op jit(solution)/shard_map/while/body/eval_jaxpr/rg,gic->ric/dot_general | solution.py:23
  189.3 11.5 %copy.9 = f32[8,256,1024]{2,1,0:T(8,128)} copy(f32[8,256,1024]{2,0,1:T(8,128)} %get-tuple-element.254) | data formatting | bytes 16777216 | tf_op jit(solution)/shard_map/while | solution.py:58
  200.9 0.6 copy-done.5
  201.4 0.6 dynamic-slice
  202.0 3.3 convert_reduce_fusion
  205.3 0.1 fusion.33
  205.5 25.3 %all-reduce = f32[8,256]{1,0:T(8,128)S(1)} all-reduce(f32[8,256]{1,0:T(8,128)S(1)} %fusion.33), channel_id=3, replica_groups=mesh['row'=8,'col'=16] {'row'}, use_global_device_ids=true, to_apply=%region_4.6.clone | all-reduce | flops 2048 | bytes 16384
  230.8 0.7 constant_dynamic-slice_fusion
  231.5 85.8 %reduce-scatter.3.cloned.1.call-done = f32[256,1024]{1,0:T(8,128)} async-done(((f32[2048,1024]{1,0:T(8,128)}), f32[256,1024]{1,0:T(8,128)}) %reduce-scatter.3.cloned.1.call-update) | async-done | bytes 1048592 | tf_op jit(solution)/shard_map/reduce_scatter | solution.py:60
  317.2 2.3 select_convert_fusion
  319.6 50.2 %all-gather.5.cloned.1.call-done = bf16[4096,1024]{1,0:T(8,128)(2,1)} async-done(((bf16[256,1024]{1,0:T(8,128)(2,1)}), bf16[4096,1024]{1,0:T(8,128)(2,1)}) %all-gather.5.cloned.1.call-update) | async-done | bytes 8388624 | tf_op jit(solution)/shard_map/all_gather | solution.py:49
  369.8 122.9 %while.29 = (s32[]{:T(128)}, f32[8,256,1024]{2,0,1:T(8,128)}, s32[32]{0:T(128)S(1)}, pred[32]{0:T(512)(128)(4,1)S(1)}, bf16[32,256,256]{2,1,0:T(8,128)(2,1)}, /*...) while((s32[]{:T(128)}, f32[8,256,1024]{2,0,1:T(8,128)}, ...), condition=%wide.region_6.8_spmd.clone, body=%wide.region_5.7_spmd.clone.sunk | while | flops 1281361024 | bytes 47190460 | solution.py:58
  369.8 0.1 compare_and_fusion.5
  369.9 6.2 gather_fusion.1
  376.1 7.1 %fusion.57 = f32[8,256,1024]{2,1,0:T(8,128)} fusion(bf16[8,256,1024]{2,1,0:T(8,128)(2,1)} %gather_fusion.1, pred[8]{0:T(512)(128)(4,1)S(1)} %get-tuple-element.429, bf16[32,256,256]{2,1,0:T(8,128)(2,1)} %get-tuple-element.489, s32[]{:T(128)S(6)} %select_n.61), kind=kOutput, calls=%fused_computation.23.clone.1 | convolution fusion | flops 1075838976 | bytes 13631500 | tf_op jit(solution)/shard_map/while/body/eval_jaxpr/gij,gjc->gic/dot_general | solution.py:19
  383.2 0.1 dynamic_slice.82
  383.2 0.1 dynamic_slice.83
  383.3 15.4 %select_add_fusion.5 = f32[8,256,1024]{2,0,1:T(8,128)} fusion(f32[8,256,1024]{2,0,1:T(8,128)} %get-tuple-element.475, pred[]{:T(512)S(6)} %compare.7, f32[8,256,1024]{2,1,0:T(8,128)} %fusion.57, s32[8]{0:T(128)S(1)} %dynamic_slice.82, pred[8]{0:T(512)(128)(4,1)S(1)} %dynamic_slice.83), kind=kOutput, calls=%fused_computation.22.clone.1 | convolution fusion | flops 205521024 | bytes 25165864 | tf_op jit(solution)/shard_map/while/body/eval_jaxpr/rg,gic->ric/dot_general | solution.py:23
  398.8 0.1 compare_and_fusion.5
  398.8 6.2 gather_fusion.1
  405.0 7.1 %fusion.57 = f32[8,256,1024]{2,1,0:T(8,128)} fusion(bf16[8,256,1024]{2,1,0:T(8,128)(2,1)} %gather_fusion.1, pred[8]{0:T(512)(128)(4,1)S(1)} %get-tuple-element.429, bf16[32,256,256]{2,1,0:T(8,128)(2,1)} %get-tuple-element.489, s32[]{:T(128)S(6)} %select_n.61), kind=kOutput, calls=%fused_computation.23.clone.1 | convolution fusion | flops 1075838976 | bytes 13631500 | tf_op jit(solution)/shard_map/while/body/eval_jaxpr/gij,gjc->gic/dot_general | solution.py:19
  412.1 0.1 dynamic_slice.82
  412.2 0.1 dynamic_slice.83
  412.2 17.8 %select_add_fusion.5 = f32[8,256,1024]{2,0,1:T(8,128)} fusion(f32[8,256,1024]{2,0,1:T(8,128)} %get-tuple-element.475, pred[]{:T(512)S(6)} %compare.7, f32[8,256,1024]{2,1,0:T(8,128)} %fusion.57, s32[8]{0:T(128)S(1)} %dynamic_slice.82, pred[8]{0:T(512)(128)(4,1)S(1)} %dynamic_slice.83), kind=kOutput, calls=%fused_computation.22.clone.1 | convolution fusion | flops 205521024 | bytes 25165864 | tf_op jit(solution)/shard_map/while/body/eval_jaxpr/rg,gic->ric/dot_general | solution.py:23
  430.1 0.1 compare_and_fusion.5
  430.2 6.2 gather_fusion.1
  436.3 7.1 %fusion.57 = f32[8,256,1024]{2,1,0:T(8,128)} fusion(bf16[8,256,1024]{2,1,0:T(8,128)(2,1)} %gather_fusion.1, pred[8]{0:T(512)(128)(4,1)S(1)} %get-tuple-element.429, bf16[32,256,256]{2,1,0:T(8,128)(2,1)} %get-tuple-element.489, s32[]{:T(128)S(6)} %select_n.61), kind=kOutput, calls=%fused_computation.23.clone.1 | convolution fusion | flops 1075838976 | bytes 13631500 | tf_op jit(solution)/shard_map/while/body/eval_jaxpr/gij,gjc->gic/dot_general | solution.py:19
  443.4 0.1 dynamic_slice.82
  443.5 0.1 dynamic_slice.83
  443.6 17.8 %select_add_fusion.5 = f32[8,256,1024]{2,0,1:T(8,128)} fusion(f32[8,256,1024]{2,0,1:T(8,128)} %get-tuple-element.475, pred[]{:T(512)S(6)} %compare.7, f32[8,256,1024]{2,1,0:T(8,128)} %fusion.57, s32[8]{0:T(128)S(1)} %dynamic_slice.82, pred[8]{0:T(512)(128)(4,1)S(1)} %dynamic_slice.83), kind=kOutput, calls=%fused_computation.22.clone.1 | convolution fusion | flops 205521024 | bytes 25165864 | tf_op jit(solution)/shard_map/while/body/eval_jaxpr/rg,gic->ric/dot_general | solution.py:23
  461.4 0.1 compare_and_fusion.5
  461.5 6.2 gather_fusion.1
  467.6 7.1 %fusion.57 = f32[8,256,1024]{2,1,0:T(8,128)} fusion(bf16[8,256,1024]{2,1,0:T(8,128)(2,1)} %gather_fusion.1, pred[8]{0:T(512)(128)(4,1)S(1)} %get-tuple-element.429, bf16[32,256,256]{2,1,0:T(8,128)(2,1)} %get-tuple-element.489, s32[]{:T(128)S(6)} %select_n.61), kind=kOutput, calls=%fused_computation.23.clone.1 | convolution fusion | flops 1075838976 | bytes 13631500 | tf_op jit(solution)/shard_map/while/body/eval_jaxpr/gij,gjc->gic/dot_general | solution.py:19
  474.8 0.1 dynamic_slice.83
  474.9 17.8 %select_add_fusion.5 = f32[8,256,1024]{2,0,1:T(8,128)} fusion(f32[8,256,1024]{2,0,1:T(8,128)} %get-tuple-element.475, pred[]{:T(512)S(6)} %compare.7, f32[8,256,1024]{2,1,0:T(8,128)} %fusion.57, s32[8]{0:T(128)S(1)} %dynamic_slice.82, pred[8]{0:T(512)(128)(4,1)S(1)} %dynamic_slice.83), kind=kOutput, calls=%fused_computation.22.clone.1 | convolution fusion | flops 205521024 | bytes 25165864 | tf_op jit(solution)/shard_map/while/body/eval_jaxpr/rg,gic->ric/dot_general | solution.py:23
  492.7 11.5 %copy.10 = f32[8,256,1024]{2,1,0:T(8,128)} copy(f32[8,256,1024]{2,0,1:T(8,128)} %get-tuple-element.255) | data formatting | bytes 16777216 | tf_op jit(solution)/shard_map/while | solution.py:58
  504.2 115.3 %reduce-scatter.5.cloned.1.call-done = f32[256,1024]{1,0:T(8,128)} async-done(((f32[2048,1024]{1,0:T(8,128)}), f32[256,1024]{1,0:T(8,128)}) %reduce-scatter.5.cloned.1.call-update) | async-done | bytes 1048592 | tf_op jit(solution)/shard_map/reduce_scatter | solution.py:60
  619.5 2.5 add_select_fusion
  (38 shorter events, 0.4 us)
Async XLA Ops:
  6.5 57.2 %all-gather.3.cloned.1.call-start = ((), (), s32[]{:S(2)}) async-start(), calls=%async_computation.2 | async-start | bytes 8912896 | tf_op jit(solution)/shard_map/all_gather | solution.py:49
  8.7 308.6 %reduce-scatter.3.cloned.1.call-start = ((), (), s32[]{:S(2)}) async-start(), calls=%async_computation.3 | async-start | bytes 9437184 | tf_op jit(solution)/shard_map/reduce_scatter | solution.py:60
  70.6 7.1 %copy-start.2 = (s32[32]{0:T(128)S(1)}, s32[32]{0:T(128)}, u32[]{:S(2)}) copy-start(s32[32]{0:T(128)} %get-tuple-element.454) | copy-start | bytes 388 | tf_op jit(solution)/shard_map/while
  100.2 7.1 %copy-start.2 = (s32[32]{0:T(128)S(1)}, s32[32]{0:T(128)}, u32[]{:S(2)}) copy-start(s32[32]{0:T(128)} %get-tuple-element.454) | copy-start | bytes 388 | tf_op jit(solution)/shard_map/while
  132.2 7.1 %copy-start.2 = (s32[32]{0:T(128)S(1)}, s32[32]{0:T(128)}, u32[]{:S(2)}) copy-start(s32[32]{0:T(128)} %get-tuple-element.454) | copy-start | bytes 388 | tf_op jit(solution)/shard_map/while
  164.2 7.1 %copy-start.2 = (s32[32]{0:T(128)S(1)}, s32[32]{0:T(128)}, u32[]{:S(2)}) copy-start(s32[32]{0:T(128)} %get-tuple-element.454) | copy-start | bytes 388 | tf_op jit(solution)/shard_map/while
  200.8 0.7 copy-start.5
  200.8 4.6 copy-start.3
  200.8 30.7 %copy-start.4 = (s32[256]{0:T(256)S(1)}, s32[256]{0:T(256)}, u32[]{:S(2)}) copy-start(s32[256]{0:T(256)} %param.17) | copy-start | bytes 3076
  200.8 116.5 %copy-start = (f32[256,1024]{1,0:T(8,128)S(1)}, f32[256,1024]{1,0:T(8,128)}, u32[]{:S(2)}) copy-start(f32[256,1024]{1,0:T(8,128)} %param.16) | copy-start | bytes 3145732
  200.8 169.1 %copy-start.1 = (s32[32]{0:T(128)S(1)}, s32[32]{0:T(128)}, u32[]{:S(2)}) copy-start(s32[32]{0:T(128)} %get-tuple-element.513) | copy-start | bytes 388
  200.8 169.0 %all-gather.5.cloned.1.call-start = ((), (), s32[]{:S(2)}) async-start(), calls=%async_computation.4 | async-start | bytes 8912896 | tf_op jit(solution)/shard_map/all_gather | solution.py:49
  319.6 299.9 %reduce-scatter.5.cloned.1.call-start = ((), (), s32[]{:S(2)}) async-start(), calls=%async_computation.5 | async-start | bytes 9437184 | tf_op jit(solution)/shard_map/reduce_scatter | solution.py:60
Sparse Core Ops, SparseCore 0:
  9.1 54.6 all-gather.2
  200.9 116.2 reduce-scatter.2
  319.7 50.0 all-gather.4
  504.3 115.1 reduce-scatter.4
where the time goes:
time: 630 us; the launch traced here: 629 us
  waiting for transfers between devices  306 us (49%)
  matrix products  195 us (31%)
  local copies, waits for them, and re-layouts  75.3 us (12%)
  blocking collectives  25.3 us (4%)
  between operations  13.9 us (2%)
  other arithmetic  13.6 us (2%)
    reduce_scatter x2, waiting for transfers between devices, on_device(): lax.psum_scatter(flat_terms, 'row', scatter_dimension=0, tiled=True)  201 us
    dot_general x8, matrix products, group_term(): jnp.einsum('rg,gic->ric', placing, product, precision=lax.Precision.HIGHEST)  138 us
    all_gather x2, waiting for transfers between devices, on_device(): lax.all_gather(current.astype(jnp.bfloat16), 'col', axis=0, tiled=True)  105 us
    dot_general x8, matrix products, group_term(): jnp.einsum('gij,gjc->gic', tile_group, fetched, preferred_element_type=jn...  56.6 us
    gather x8, local copies, waits for them, and re-layouts, group_term(): fetched = jnp.take(gathered, group_cols, axis=0)  49.3 us
    unnamed x1, blocking collectives  25.3 us
    while x2, local copies, waits for them, and re-layouts, on_device(): running = lax.fori_loop(0, group_total, add_group, empty)  22.9 us
  transfers between devices with their start and end apart: 4, of which 4 were waited for; matrix products, arithmetic and copies ran while one was open for 1% of the time, Pallas kernels for 0%

commit v1 on v0

v1 whole, which is shorter than its diff:
```python
import jax
import jax.numpy as jnp
from jax import lax
from jax.experimental import pallas as pl
from jax.experimental.pallas import tpu as pltpu
from jax.sharding import PartitionSpec as P

MESH = pl.DeviceIdType.MESH
SWEEPS = 2
CHUNKS = 4
STRIP = 64
SPREAD = 0.8

PER_NAT = 2048.0 / 0.6931471805599453
ONE_CODE = 32700.0
LEAST = -32768.0


def encode(v):
    code = jnp.log(jnp.maximum(v, 1e-30)) * PER_NAT + ONE_CODE
    code = jnp.minimum(jnp.maximum(code, LEAST), 32767.0)
    return jnp.floor(code + 0.5).astype(jnp.int32).astype(jnp.int16)


def decode(q):
    code = q.astype(jnp.int32).astype(jnp.float32)
    v = jnp.exp((code - ONE_CODE) * (1.0 / PER_NAT))
    return jnp.where(code > LEAST, v, 0.0)


def make_kernel(sizes):
    slots, bs, classes, rows_n, cols_n = sizes
    width = classes // CHUNKS
    half = bs // 2
    steps = SWEEPS * CHUNKS

    def kernel(rows_s, cols_s, count_s, aff, labels, marked, out, wv, sums, deg_run, deg_all, inv, mask, prev_s, last_s,
               kept, *rest):
        xs = rest[:steps]
        outs = [rest[steps + 14 * q : steps + 14 * q + 7] for q in range(steps)]
        ins = [rest[steps + 14 * q + 7 : steps + 14 * q + 14] for q in range(steps)]
        (w_sem, xl_sem, z_sem, zr_sem, sib_sem, ag_send, rl_sem, nb_sem, xh_sem, rs_send, dg_recv, dg_send) = rest[15 * steps :]

        r, c = lax.axis_index("row"), lax.axis_index("col")
        y, xh = r // 2, r % 2
        xl, z, core = c // 8, (c // 2) % 4, c % 2
        zs = [(z + k) % 4 for k in range(4)]
        ys = [(y + k) % 4 for k in range(4)]
        col_of = lambda a, b, k: a * 8 + b * 2 + k
        sib = (r, col_of(xl, z, 1 - core))
        far_xl = (r, col_of(1 - xl, z, core))
        z_to = ((r, col_of(xl, zs[1], core)), (r, col_of(xl, zs[3], core)))
        y_to = ((ys[1] * 2 + xh, c), (ys[3] * 2 + xh, c))
        xh_to = (y * 2 + 1 - xh, c)
        rows_to = [((r + k) % rows_n, c) for k in range(1, rows_n)]

        barrier = pltpu.get_barrier_semaphore()
        met = [sib, far_xl, *z_to, *rows_to]
        for device in met:
            pl.semaphore_signal(barrier, inc=1, device_id=device, device_id_type=MESH)
        pl.semaphore_wait(barrier, len(met))

        def copy(src, dst, send, recv, device):
            return pltpu.make_async_remote_copy(
                src_ref=src, dst_ref=dst, send_sem=send, recv_sem=recv, device_id=device, device_id_type=MESH
            )

        def put(q, ref, recv, device):
            copy(ref, ref, ag_send.at[q], recv, device).start()

        def got(q, ref, recv, device):
            copy(ref, ref, ag_send.at[q], recv, device).wait_recv()

        def gather_own(q):
            own = xs[q].at[c]
            put(q, own, xl_sem.at[q], far_xl)
            put(q, own, z_sem.at[q, 0, 0], z_to[0])
            put(q, own, z_sem.at[q, 0, 1], z_to[1])
            put(q, own, sib_sem.at[q, 0], sib)

        def gather_pair(q):
            block = xs[q].at[col_of(1 - xl, z, core)]
            got(q, block, xl_sem.at[q], far_xl)
            put(q, block, z_sem.at[q, 1, 0], z_to[0])
            put(q, block, z_sem.at[q, 1, 1], z_to[1])
            put(q, block, sib_sem.at[q, 1], sib)

        def gather_near(q):
            for kind in (0, 1):
                side = xl if kind == 0 else 1 - xl
                for d in (0, 1):
                    b = col_of(side, zs[3] if d == 0 else zs[1], core)
                    got(q, xs[q].at[b], z_sem.at[q, kind, d], z_to[d])
                    put(q, xs[q].at[b, pl.ds(half * d, half)], zr_sem.at[q, kind, d], z_to[d])
                    put(q, xs[q].at[b], sib_sem.at[q, 2 + 2 * kind + d], sib)

        def gather_far(q):
            for kind in (0, 1):
                b = col_of(xl if kind == 0 else 1 - xl, zs[2], core)
                for d in (0, 1):
                    part = xs[q].at[b, pl.ds(half * d, half)]
                    got(q, part, zr_sem.at[q, kind, d], z_to[d])
                    put(q, part, sib_sem.at[q, 6 + 2 * kind + d], sib)

        def gather_sibling(q):
            for kind in (0, 1):
                side = xl if kind == 0 else 1 - xl
                got(q, xs[q].at[col_of(side, z, 1 - core)], sib_sem.at[q, kind], sib)
                for d in (0, 1):
                    near = xs[q].at[col_of(side, zs[3] if d == 0 else zs[1], 1 - core)]
                    got(q, near, sib_sem.at[q, 2 + 2 * kind + d], sib)
                    far = xs[q].at[col_of(side, zs[2], 1 - core), pl.ds(half * d, half)]
                    got(q, far, sib_sem.at[q, 6 + 2 * kind + d], sib)

        def products(q):
            def four(i, _):
                for k in range(4):
                    s = i * 4 + k
                    block = xs[q][cols_s[0, 0, s]]
                    sums[s + 1] = sums[prev_s[s]] + jnp.dot(wv[s], block, preferred_element_type=jnp.float32)
                return 0

            lax.fori_loop(0, slots // 4, four, 0)

        def share(rho, first):
            scale = inv[rho, pl.ds(first, STRIP), :]
            scale = jnp.concatenate([scale] * (width // 128), axis=1)
            return sums[last_s[rho], pl.ds(first, STRIP), :] * scale

        per_half = half // STRIP

        def strips(count, body):
            def step(i, _):
                body(i)
                return 0

            lax.fori_loop(0, count, step, 0)

        def send_unit(q, unit, recv, device):
            copy(outs[q][unit], ins[q][unit], rs_send.at[q, unit], recv, device).start()

        def got_unit(q, unit, recv, device):
            copy(outs[q][unit], ins[q][unit], rs_send.at[q, unit], recv, device).wait_recv()

        def sums_first(q):
            for h in (0, 1):
                def relay(i):
                    side, first = i // per_half, (i % per_half) * STRIP
                    value = share(ys[2] * 2 + side, h * half + first)
                    outs[q][h][pl.ds(i * STRIP, STRIP), :] = encode(value)

                strips(2 * per_half, relay)
                send_unit(q, h, rl_sem.at[q, h], y_to[h])
            for d in (0, 1):
                def straight(i):
                    side, first = i // per_half, (i % per_half) * STRIP
                    value = share((ys[1] if d == 0 else ys[3]) * 2 + side, (1 - d) * half + first)
                    outs[q][2 + 2 * d + 1 - d][pl.ds(i * STRIP, STRIP), :] = encode(value)

                strips(2 * per_half, straight)
                send_unit(q, 2 + 2 * d + 1 - d, nb_sem.at[q, d, 1 - d], y_to[d])

        def sums_relay(q):
            for d in (0, 1):
                got_unit(q, d, rl_sem.at[q, d], y_to[d])

                def joined(i):
                    side, first = i // per_half, (i % per_half) * STRIP
                    value = share((ys[1] if d == 0 else ys[3]) * 2 + side, d * half + first)
                    at = pl.ds(i * STRIP, STRIP)
                    outs[q][2 + 2 * d + d][at, :] = encode(value + decode(ins[q][d][at, :]))

                strips(2 * per_half, joined)
                send_unit(q, 2 + 2 * d + d, nb_sem.at[q, d, d], y_to[d])

        def in_y(q, side, h, first):
            at = pl.ds(side * half + first, STRIP)
            value = share(y * 2 + side, h * half + first) + decode(ins[q][2 + h][at, :])
            return value + decode(ins[q][4 + h][at, :])

        def sums_y(q):
            for h in (0, 1):
                for d in (0, 1):
                    got_unit(q, 2 + 2 * d + h, nb_sem.at[q, d, h], y_to[d])
            for h in (0, 1):
                def other(i):
                    outs[q][6][pl.ds(h * half + i * STRIP, STRIP), :] = encode(in_y(q, 1 - xh, h, i * STRIP))

                strips(per_half, other)
            send_unit(q, 6, xh_sem.at[q], xh_to)
            for h in (0, 1):
                def own(i):
                    kept[pl.ds(h * half + i * STRIP, STRIP), :] = in_y(q, xh, h, i * STRIP)

                strips(per_half, own)

        def sums_x(q):
            got_unit(q, 6, xh_sem.at[q], xh_to)
            lanes = pl.ds((q % CHUNKS) * width, width)

            def finish(i):
                at = pl.ds(i * STRIP, STRIP)
                total = kept[at, :] + decode(ins[q][6][at, :])
                prior = labels[at, lanes]
                keep = jnp.concatenate([mask[at, :]] * (width // 128), axis=1)
                value = jnp.where(keep == 1.0, prior, SPREAD * total + (1.0 - SPREAD) * prior)
                if q < steps - CHUNKS:
                    xs[q + CHUNKS][c, at, :] = value.astype(jnp.bfloat16)
                else:
                    out[at, lanes] = value

            strips(2 * per_half, finish)
            if q < steps - CHUNKS:
                gather_own(q + CHUNKS)

        load = pltpu.make_async_copy(aff.at[0, 0], wv, w_sem)
        load.start()

        def first_scores(q):
            def cast(i):
                at = pl.ds(i * STRIP, STRIP)
                xs[q][c, at, :] = labels[at, pl.ds(q * width, width)].astype(jnp.bfloat16)

            strips(bs // STRIP, cast)
            gather_own(q)

        first_scores(0)
        live = count_s[0, 0]

        def chain(s, lasts):
            row = rows_s[0, 0, s]
            before = jnp.int32(0)
            new = []
            for rho in range(rows_n):
                before = jnp.where(row == rho, lasts[rho], before)
                new.append(jnp.where((row == rho) & (s < live), s + 1, lasts[rho]))
            prev_s[s] = before
            return tuple(new)

        lasts = lax.fori_loop(0, slots, chain, (jnp.int32(0),) * rows_n)
        for rho in range(rows_n):
            last_s[rho] = lasts[rho]
        sums[0] = jnp.zeros((bs, width), jnp.float32)
        deg_run[0] = jnp.zeros((8, bs), jnp.float32)
        gather_pair(0)
        first_scores(1)

        load.wait()

        def row_sums(i, _):
            ones = jnp.ones((8, bs), jnp.bfloat16)
            for k in range(4):
                s = i * 4 + k
                part = lax.dot_general(ones, wv[s], (((1,), (1,)), ((), ())), preferred_element_type=jnp.float32)
                deg_run[s + 1] = deg_run[prev_s[s]] + part
            return 0

        lax.fori_loop(0, slots // 4, row_sums, 0)
        for rho in range(rows_n):
            deg_all[r, pl.ds(rho, 1), :] = deg_run[last_s[rho], pl.ds(0, 1), :]
        for k, device in enumerate(rows_to):
            copy(deg_all.at[r], deg_all.at[r], dg_send, dg_recv.at[k], device).start()

        def degrees():
            for k in range(1, rows_n):
                block = deg_all.at[(r + rows_n - k) % rows_n]
                copy(block, block, dg_send, dg_recv.at[k - 1], rows_to[k - 1]).wait_recv()
            degree = deg_all[0]
            for k in range(1, rows_n):
                degree = degree + deg_all[k]
            marks = jnp.broadcast_to(marked[...].astype(jnp.float32), (8, bs))
            stack = jnp.concatenate([1.0 / degree, marks, jnp.zeros((112, bs), jnp.float32)], axis=0)
            turned = jnp.transpose(stack)
            for rho in range(rows_n):
                inv[rho] = jnp.broadcast_to(turned[:, rho : rho + 1], (bs, 128))
            mask[...] = jnp.broadcast_to(turned[:, rows_n : rows_n + 1], (bs, 128))

        for q in range(steps):
            if q > 0:
                gather_pair(q)
                sums_relay(q - 1)
            gather_near(q)
            if q > 0:
                if q + 1 < CHUNKS:
                    first_scores(q + 1)
                sums_y(q - 1)
            gather_far(q)
            if q > 0:
                sums_x(q - 1)
            gather_sibling(q)
            products(q)
            if q == 0:
                degrees()
            sums_first(q)
        sums_relay(steps - 1)
        sums_y(steps - 1)
        sums_x(steps - 1)

        for q in range(steps):
            sent = xs[q].at[pl.ds(0, 15)]
            copy(sent, sent, ag_send.at[q], xl_sem.at[q], sib).wait_send()
            for unit in range(7):
                copy(outs[q][unit], ins[q][unit], rs_send.at[q, unit], xh_sem.at[q], xh_to).wait_send()
        copy(deg_all.at[pl.ds(0, rows_n - 1)], deg_all.at[pl.ds(0, rows_n - 1)], dg_send, dg_recv.at[0], rows_to[0]).wait_send()

    return kernel


def solution(mesh):
    rows_n, cols_n = mesh.shape["row"], mesh.shape["col"]

    def on_device(affinity, block_rows, block_cols, block_count, labels, labelled):
        slots, bs = affinity.shape[2], affinity.shape[3]
        classes = labels.shape[1]
        width = classes // CHUNKS
        half = bs // 2
        steps = SWEEPS * CHUNKS
        dma = pltpu.SemaphoreType.DMA
        scratch = [
            pltpu.VMEM((slots, bs, bs), jnp.bfloat16),
            pltpu.VMEM((slots + 1, bs, width), jnp.float32),
            pltpu.VMEM((slots + 1, 8, bs), jnp.float32),
            pltpu.VMEM((rows_n, rows_n, bs), jnp.float32),
            pltpu.VMEM((rows_n, bs, 128), jnp.float32),
            pltpu.VMEM((bs, 128), jnp.float32),
            pltpu.SMEM((slots,), jnp.int32),
            pltpu.SMEM((rows_n,), jnp.int32),
            pltpu.VMEM((bs, width), jnp.float32),
            *[pltpu.VMEM((cols_n, bs, width), jnp.bfloat16)] * steps,
            *[pltpu.VMEM((bs, width), jnp.int16)] * (14 * steps),
            dma,
            dma((steps,)),
            dma((steps, 2, 2)),
            dma((steps, 2, 2)),
            dma((steps, 10)),
            dma((steps,)),
            dma((steps, 2)),
            dma((steps, 2, 2)),
            dma((steps,)),
            dma((steps, 7)),
            dma((rows_n - 1,)),
            dma,
        ]
        smem = pl.BlockSpec(memory_space=pltpu.SMEM)
        vmem = pl.BlockSpec(memory_space=pltpu.VMEM)
        return pl.pallas_call(
            make_kernel((slots, bs, classes, rows_n, cols_n)),
            out_shape=jax.ShapeDtypeStruct(labels.shape, jnp.float32),
            in_specs=[smem, smem, smem, pl.BlockSpec(memory_space=pl.ANY), vmem, vmem],
            out_specs=vmem,
            scratch_shapes=scratch,
            compiler_params=pltpu.CompilerParams(
                collective_id=0, has_side_effects=True, vmem_limit_bytes=60 * 1024 * 1024
            ),
        )(block_rows, block_cols, block_count, affinity, labels, labelled.reshape(1, bs))

    placed = (
        P("row", "col", None, None, None),
        P("row", "col", None),
        P("row", "col", None),
        P("row", "col"),
        P(("row", "col"), None),
        P(("row", "col")),
    )
    return jax.shard_map(
        on_device, mesh=mesh, in_specs=placed, out_specs=P(("row", "col"), None), check_vma=False
    )
```

time: 630 us -> 181 us (0.29)
  waiting for transfers between devices: 306 us -> 0 us
  matrix products: 195 us -> 0 us
  Pallas kernels: 0 us -> 177 us
  local copies, waits for them, and re-layouts: 75.3 us -> 2.31 us
  blocking collectives: 25.3 us -> 0 us
  other arithmetic: 13.6 us -> 0 us
  between operations: 13.9 us -> 0.66 us
    reduce_scatter x2 -> x0, waiting for transfers between devices: 201 us -> none  [on_device(): lax.psum_scatter(flat_terms, 'row', scatter_dimension=0, tiled=True)]
    dot_general x17 -> x0, matrix products: 195 us -> none  [the longest x8 138 us: group_term(): jnp.einsum('rg,gic->ric', placing, product, precision=lax.Precision.HIGHEST)]
    pallas_call x0 -> x1, Pallas kernels: none -> 177 us  [on_device(): pl.pallas_call(make_kernel((slots, bs, classes, rows_n, cols_n)), out_sha...]
    all_gather x2 -> x0, waiting for transfers between devices: 105 us -> none  [on_device(): lax.all_gather(current.astype(jnp.bfloat16), 'col', axis=0, tiled=True)]
    gather x8 -> x0, local copies, waits for them, and re-layouts: 49.3 us -> none  [group_term(): fetched = jnp.take(gathered, group_cols, axis=0)]
    unnamed x1 -> x0, blocking collectives: 25.3 us -> none
    while x10 -> x0, local copies, waits for them, and re-layouts: 22.9 us -> none  [the longest x2 22.9 us: on_device(): running = lax.fori_loop(0, group_total, add_group, empty)]
  transfers between devices with their start and end apart: 4 -> 0, of which waited for: 4 -> 0; matrix products, arithmetic and copies ran while one was open for 1% -> 0% of each run, Pallas kernels for 0% -> 0%
where the time goes in v1:
time: 181 us; the launch traced here: 180 us
  Pallas kernels  177 us (98%)
  local copies, waits for them, and re-layouts  2.31 us (1%)
    pallas_call x1, Pallas kernels, on_device(): pl.pallas_call(make_kernel((slots, bs, classes, rows_n, cols_n)), out_sha...  177 us

profile of v1, /device:TPU:0, one launch (start us, length us, event | category | flops | bytes accessed | tf_op | source)
XLA Modules:
  0.0 179.9 jit_solution(18021079774247219550)
XLA Ops:
  0.7 177.0 %shard_map.64 = f32[256,1024]{1,0:T(8,128)} custom-call(s32[1,1,32]{2,1,0:T(1,128)} %rows_s.1, s32[1,1,32]{2,1,0:T(1,128)} %cols_s.1, s32[1,1]{1,0:T(1,128)S(6)} %copy.8.count_s, bf16[1,1,32,256,256]{4,3,2,1,0:T(8,128)(2,1)} %aff.1, f32[256,1024]{1,0:T(8,128)} %labels.1, s32[1,256]{1,0:T(1,128)} %bitcast.1), custom_call_target="tpu_custom_call" | custom-call | tf_op jit(solution)/shard_map/pallas_call | solution.py:346
  177.6 2.3 %copy.9 = f32[256,1024]{1,0:T(8,128)} copy(f32[256,1024]{1,0:T(8,128)} %shard_map.64) | data formatting | bytes 2097152

commit v2 on v0

v2 whole, which is shorter than its diff:
```python
import jax
import jax.numpy as jnp
from jax import lax
from jax.experimental import pallas as pl
from jax.experimental.pallas import tpu as pltpu
from jax.sharding import PartitionSpec as P

MESH = pl.DeviceIdType.MESH
SWEEPS = 2
WIDTHS = (256, 256, 256, 256)
PIECES = 2
STRIP = 64
SPREAD = 0.8

ORDER = (
    2000, 2010, 0, 3000, 4001, 4000, 4002, 4003, 4011, 4010, 1000, 5001, 5000, 3010, 2020, 5002, 5003, 6000,
    6001, 7000, 7001, 5011, 4013, 5010, 8001, 4012, 3020, 8000, 2030, 4021, 9000, 5013, 5012, 4020, 10000,
    10001, 6010, 6011, 7010, 7011, 4023, 4022, 3030, 4030, 11000, 8010, 5021, 9010, 8011, 5023, 5022, 4031,
    5020, 10010, 10011, 6020, 4032, 4033, 12000, 2040, 6021, 7020, 7021, 5033, 8021, 5030, 11010, 5032, 5031,
    9020, 8020, 3040, 6030, 4040, 4041, 10020, 10021, 6031, 12010, 2050, 4043, 7030, 8030, 4042, 5040, 5041,
    7031, 8031, 11020, 3050, 4051, 9030, 4050, 10030, 5042, 5043, 10031, 6040, 12020, 2060, 6041, 7040, 7041,
    4052, 4053, 8040, 11030, 9040, 5051, 8041, 5050, 4061, 4060, 5052, 5053, 3060, 10040, 10041, 6050, 12030,
    2070, 6051, 5061, 7050, 7051, 8051, 4062, 4063, 3070, 8050, 4071, 5060, 4070, 11040, 9050, 5063, 5062,
    10050, 10051, 6060, 4072, 4073, 6061, 7060, 7061, 9060, 5071, 5070, 8060, 8061, 5072, 5073, 6070, 10060,
    10061, 6071, 7071, 7070, 8070, 12040, 9070, 8071, 11050, 11060, 10070, 10071, 11070, 12060, 12050, 12070,
)

PER_NAT = 2048.0 / 0.6931471805599453
ONE_CODE = 32700.0
LEAST = -32768.0


def encode(v):
    code = jnp.log(jnp.maximum(v, 1e-30)) * PER_NAT + ONE_CODE
    code = jnp.minimum(jnp.maximum(code, LEAST), 32767.0)
    return jnp.floor(code + 0.5).astype(jnp.int32).astype(jnp.int16)


def decode(q):
    code = q.astype(jnp.int32).astype(jnp.float32)
    v = jnp.exp((code - ONE_CODE) * (1.0 / PER_NAT))
    return jnp.where(code > LEAST, v, 0.0)


def make_kernel(sizes):
    slots, bs, rows_n, cols_n = sizes
    chunks = len(WIDTHS)
    half = bs // 2
    steps = SWEEPS * chunks
    per_half = half // STRIP

    def kernel(rows_s, cols_s, count_s, aff, labels, marked, out, wv, sums, deg_run, deg_all, inv, mask, prev_s, last_s, *rest):
        xs = rest[:steps]
        pend = rest[steps : 2 * steps]
        outs = [rest[2 * steps + 14 * q : 2 * steps + 14 * q + 7] for q in range(steps)]
        ins = [rest[2 * steps + 14 * q + 7 : 2 * steps + 14 * q + 14] for q in range(steps)]
        (w_sem, xl_sem, z_sem, zr_sem, sib_sem, ag_send, rl_sem, nb_sem, xh_sem, rs_send, dg_recv, dg_send) = rest[16 * steps :]

        r, c = lax.axis_index("row"), lax.axis_index("col")
        y, xh = r // 2, r % 2
        xl, z, core = c // 8, (c // 2) % 4, c % 2
        zs = [(z + k) % 4 for k in range(4)]
        ys = [(y + k) % 4 for k in range(4)]
        col_of = lambda a, b, k: a * 8 + b * 2 + k
        sib = (r, col_of(xl, z, 1 - core))
        far_xl = (r, col_of(1 - xl, z, core))
        z_to = ((r, col_of(xl, zs[1], core)), (r, col_of(xl, zs[3], core)))
        y_to = ((ys[1] * 2 + xh, c), (ys[3] * 2 + xh, c))
        xh_to = (y * 2 + 1 - xh, c)
        rows_to = [((r + k) % rows_n, c) for k in range(1, rows_n)]

        barrier = pltpu.get_barrier_semaphore()
        met = [sib, far_xl, *z_to, *rows_to]
        for device in met:
            pl.semaphore_signal(barrier, inc=1, device_id=device, device_id_type=MESH)
        load = pltpu.make_async_copy(aff.at[0, 0], wv, w_sem)
        load.start()
        pl.semaphore_wait(barrier, len(met))

        def width(q):
            return WIDTHS[q % chunks]

        def lanes(q):
            return pl.ds(sum(WIDTHS[: q % chunks]), width(q))

        def copy(src, dst, send, recv, device):
            return pltpu.make_async_remote_copy(
                src_ref=src, dst_ref=dst, send_sem=send, recv_sem=recv, device_id=device, device_id_type=MESH
            )

        def strips(count, body):
            def step(i, _):
                body(i)
                return 0

            lax.fori_loop(0, count, step, 0)

        def put(q, ref, recv, device):
            copy(ref, ref, ag_send.at[q], recv, device).start()

        def got(q, ref, recv, device):
            copy(ref, ref, ag_send.at[q], recv, device).wait_recv()

        def own(q):
            if q < chunks:
                def cast(i):
                    at = pl.ds(i * STRIP, STRIP)
                    xs[q][c, at, :] = labels[at, lanes(q)].astype(jnp.bfloat16)

                strips(bs // STRIP, cast)
            block = xs[q].at[c]
            put(q, block, xl_sem.at[q], far_xl)
            put(q, block, z_sem.at[q, 0, 0], z_to[0])
            put(q, block, z_sem.at[q, 0, 1], z_to[1])
            put(q, block, sib_sem.at[q, 0], sib)

        def pair(q):
            block = xs[q].at[col_of(1 - xl, z, core)]
            got(q, block, xl_sem.at[q], far_xl)
            put(q, block, z_sem.at[q, 1, 0], z_to[0])
            put(q, block, z_sem.at[q, 1, 1], z_to[1])
            put(q, block, sib_sem.at[q, 1], sib)

        def near(q, kind, d):
            b = col_of(xl if kind == 0 else 1 - xl, zs[3] if d == 0 else zs[1], core)
            got(q, xs[q].at[b], z_sem.at[q, kind, d], z_to[d])
            put(q, xs[q].at[b, pl.ds(half * d, half)], zr_sem.at[q, kind, d], z_to[d])
            put(q, xs[q].at[b], sib_sem.at[q, 2 + 2 * kind + d], sib)

        def far(q, kind, d):
            b = col_of(xl if kind == 0 else 1 - xl, zs[2], core)
            part = xs[q].at[b, pl.ds(half * d, half)]
            got(q, part, zr_sem.at[q, kind, d], z_to[d])
            put(q, part, sib_sem.at[q, 6 + 2 * kind + d], sib)

        def from_sibling(q):
            for kind in (0, 1):
                side = xl if kind == 0 else 1 - xl
                got(q, xs[q].at[col_of(side, z, 1 - core)], sib_sem.at[q, kind], sib)
                for d in (0, 1):
                    block = xs[q].at[col_of(side, zs[3] if d == 0 else zs[1], 1 - core)]
                    got(q, block, sib_sem.at[q, 2 + 2 * kind + d], sib)
                    part = xs[q].at[col_of(side, zs[2], 1 - core), pl.ds(half * d, half)]
                    got(q, part, sib_sem.at[q, 6 + 2 * kind + d], sib)

        def prod(q, piece):
            if piece == 0:
                from_sibling(q)
            wide = pl.ds(0, width(q))
            first = piece * (slots // PIECES)

            def four(i, _):
                for k in range(4):
                    s = first + i * 4 + k
                    block = xs[q][cols_s[0, 0, s]]
                    sums[s + 1, :, wide] = sums[prev_s[s], :, wide] + jnp.dot(wv[s], block, preferred_element_type=jnp.float32)
                return 0

            lax.fori_loop(0, slots // PIECES // 4, four, 0)

        def share(q, rho, first):
            scale = inv[rho, pl.ds(first, STRIP), :]
            scale = jnp.concatenate([scale] * (width(q) // 128), axis=1)
            return sums[last_s[rho], pl.ds(first, STRIP), pl.ds(0, width(q))] * scale

        def send_unit(q, unit, recv, device):
            copy(outs[q][unit], ins[q][unit], rs_send.at[q, unit], recv, device).start()

        def got_unit(q, unit, recv, device):
            copy(outs[q][unit], ins[q][unit], rs_send.at[q, unit], recv, device).wait_recv()

        def send_far(q, h):
            def relay(i):
                side, first = i // per_half, (i % per_half) * STRIP
                outs[q][h][pl.ds(i * STRIP, STRIP), :] = encode(share(q, ys[2] * 2 + side, h * half + first))

            strips(2 * per_half, relay)
            send_unit(q, h, rl_sem.at[q, h], y_to[h])

        def send_near(q, d):
            unit = 3 if d == 0 else 4

            def straight(i):
                side, first = i // per_half, (i % per_half) * STRIP
                value = share(q, (ys[1] if d == 0 else ys[3]) * 2 + side, (1 - d) * half + first)
                outs[q][unit][pl.ds(i * STRIP, STRIP), :] = encode(value)

            strips(2 * per_half, straight)
            send_unit(q, unit, nb_sem.at[q, d, 1 - d], y_to[d])

        def set_aside(q):
            for d in (0, 1):
                def wait_relay(i):
                    side, first = i // per_half, (i % per_half) * STRIP
                    value = share(q, (ys[1] if d == 0 else ys[3]) * 2 + side, d * half + first)
                    pend[q][pl.ds(d * bs + i * STRIP, STRIP), :] = value

                strips(2 * per_half, wait_relay)
            for side in (0, 1):
                def stay(i):
                    pend[q][pl.ds((2 + side) * bs + i * STRIP, STRIP), :] = share(q, y * 2 + side, i * STRIP)

                strips(2 * per_half, stay)

        def relay_on(q, d):
            unit = 2 if d == 0 else 5
            got_unit(q, d, rl_sem.at[q, d], y_to[d])

            def joined(i):
                at = pl.ds(i * STRIP, STRIP)
                value = pend[q][pl.ds(d * bs + i * STRIP, STRIP), :] + decode(ins[q][d][at, :])
                outs[q][unit][at, :] = encode(value)

            strips(2 * per_half, joined)
            send_unit(q, unit, nb_sem.at[q, d, d], y_to[d])

        def in_y(q, side, h, first):
            at = pl.ds(side * half + first, STRIP)
            value = pend[q][pl.ds((2 + side) * bs + h * half + first, STRIP), :] + decode(ins[q][2 + h][at, :])
            return value + decode(ins[q][4 + h][at, :])

        def over_y(q):
            for h in (0, 1):
                for d in (0, 1):
                    got_unit(q, 2 + 2 * d + h, nb_sem.at[q, d, h], y_to[d])
            for h in (0, 1):
                def other(i):
                    outs[q][6][pl.ds(h * half + i * STRIP, STRIP), :] = encode(in_y(q, 1 - xh, h, i * STRIP))

                strips(per_half, other)
            send_unit(q, 6, xh_sem.at[q], xh_to)
            for h in (0, 1):
                def mine(i):
                    value = in_y(q, xh, h, i * STRIP)
                    pend[q][pl.ds((2 + xh) * bs + h * half + i * STRIP, STRIP), :] = value

                strips(per_half, mine)

        def finish(q):
            got_unit(q, 6, xh_sem.at[q], xh_to)

            def update(i):
                at = pl.ds(i * STRIP, STRIP)
                total = pend[q][pl.ds((2 + xh) * bs + i * STRIP, STRIP), :] + decode(ins[q][6][at, :])
                prior = labels[at, lanes(q)]
                keep = jnp.concatenate([mask[at, :]] * (width(q) // 128), axis=1)
                value = jnp.where(keep == 1.0, prior, SPREAD * total + (1.0 - SPREAD) * prior)
                if q < steps - chunks:
                    xs[q + chunks][c, at, :] = value.astype(jnp.bfloat16)
                else:
                    out[at, lanes(q)] = value

            strips(2 * per_half, update)

        def degrees_out(q):
            live = count_s[0, 0]

            def chain(s, lasts):
                row = rows_s[0, 0, s]
                before = jnp.int32(0)
                new = []
                for rho in range(rows_n):
                    before = jnp.where(row == rho, lasts[rho], before)
                    new.append(jnp.where((row == rho) & (s < live), s + 1, lasts[rho]))
                prev_s[s] = before
                return tuple(new)

            lasts = lax.fori_loop(0, slots, chain, (jnp.int32(0),) * rows_n)
            for rho in range(rows_n):
                last_s[rho] = lasts[rho]
            sums[0] = jnp.zeros((bs, max(WIDTHS)), jnp.float32)
            deg_run[0] = jnp.zeros((8, bs), jnp.float32)
            load.wait()

            def row_sums(i, _):
                ones = jnp.ones((8, bs), jnp.bfloat16)
                for k in range(4):
                    s = i * 4 + k
                    part = lax.dot_general(ones, wv[s], (((1,), (1,)), ((), ())), preferred_element_type=jnp.float32)
                    deg_run[s + 1] = deg_run[prev_s[s]] + part
                return 0

            lax.fori_loop(0, slots // 4, row_sums, 0)
            for rho in range(rows_n):
                deg_all[r, pl.ds(rho, 1), :] = deg_run[last_s[rho], pl.ds(0, 1), :]
            for k, device in enumerate(rows_to):
                copy(deg_all.at[r], deg_all.at[r], dg_send, dg_recv.at[k], device).start()

        def degrees_in(q):
            for k in range(1, rows_n):
                block = deg_all.at[(r + rows_n - k) % rows_n]
                copy(block, block, dg_send, dg_recv.at[k - 1], rows_to[k - 1]).wait_recv()
            degree = deg_all[0]
            for k in range(1, rows_n):
                degree = degree + deg_all[k]
            marks = jnp.broadcast_to(marked[...].astype(jnp.float32), (8, bs))
            stack = jnp.concatenate([1.0 / degree, marks, jnp.zeros((112, bs), jnp.float32)], axis=0)
            turned = jnp.transpose(stack)
            for rho in range(rows_n):
                inv[rho] = jnp.broadcast_to(turned[:, rho : rho + 1], (bs, 128))
            mask[...] = jnp.broadcast_to(turned[:, rows_n : rows_n + 1], (bs, 128))

        phases = (degrees_out, degrees_in, own, pair, near, far, prod, send_far, send_near, set_aside, relay_on, over_y, finish)
        for code in ORDER:
            kind, q, more = code // 1000, code // 10 % 100, code % 10
            if kind in (4, 5):
                phases[kind](q, more // 2, more % 2)
            elif kind in (6, 7, 8, 10):
                phases[kind](q, more)
            else:
                phases[kind](q)

        for q in range(steps):
            sent = xs[q].at[pl.ds(0, 15)]
            copy(sent, sent, ag_send.at[q], xl_sem.at[q], sib).wait_send()
            for unit in range(7):
                copy(outs[q][unit], ins[q][unit], rs_send.at[q, unit], xh_sem.at[q], xh_to).wait_send()
        copy(deg_all.at[pl.ds(0, rows_n - 1)], deg_all.at[pl.ds(0, rows_n - 1)], dg_send, dg_recv.at[0], rows_to[0]).wait_send()

    return kernel


def solution(mesh):
    rows_n, cols_n = mesh.shape["row"], mesh.shape["col"]

    def on_device(affinity, block_rows, block_cols, block_count, labels, labelled):
        slots, bs = affinity.shape[2], affinity.shape[3]
        steps = SWEEPS * len(WIDTHS)
        each = WIDTHS * SWEEPS
        dma = pltpu.SemaphoreType.DMA
        scratch = [
            pltpu.VMEM((slots, bs, bs), jnp.bfloat16),
            pltpu.VMEM((slots + 1, bs, max(WIDTHS)), jnp.float32),
            pltpu.VMEM((slots + 1, 8, bs), jnp.float32),
            pltpu.VMEM((rows_n, rows_n, bs), jnp.float32),
            pltpu.VMEM((rows_n, bs, 128), jnp.float32),
            pltpu.VMEM((bs, 128), jnp.float32),
            pltpu.SMEM((slots,), jnp.int32),
            pltpu.SMEM((rows_n,), jnp.int32),
            *[pltpu.VMEM((cols_n, bs, width), jnp.bfloat16) for width in each],
            *[pltpu.VMEM((4 * bs, width), jnp.float32) for width in each],
            *[pltpu.VMEM((bs, width), jnp.int16) for width in each for _ in range(14)],
            dma,
            dma((steps,)),
            dma((steps, 2, 2)),
            dma((steps, 2, 2)),
            dma((steps, 10)),
            dma((steps,)),
            dma((steps, 2)),
            dma((steps, 2, 2)),
            dma((steps,)),
            dma((steps, 7)),
            dma((rows_n - 1,)),
            dma,
        ]
        smem = pl.BlockSpec(memory_space=pltpu.SMEM)
        vmem = pl.BlockSpec(memory_space=pltpu.VMEM)
        return pl.pallas_call(
            make_kernel((slots, bs, rows_n, cols_n)),
            out_shape=jax.ShapeDtypeStruct(labels.shape, jnp.float32),
            in_specs=[smem, smem, smem, pl.BlockSpec(memory_space=pl.ANY), vmem, vmem],
            out_specs=vmem,
            scratch_shapes=scratch,
            compiler_params=pltpu.CompilerParams(
                collective_id=0, has_side_effects=True, vmem_limit_bytes=60 * 1024 * 1024
            ),
        )(block_rows, block_cols, block_count, affinity, labels, labelled.reshape(1, bs))

    placed = (
        P("row", "col", None, None, None),
        P("row", "col", None),
        P("row", "col", None),
        P("row", "col"),
        P(("row", "col"), None),
        P(("row", "col")),
    )
    return jax.shard_map(
        on_device, mesh=mesh, in_specs=placed, out_specs=P(("row", "col"), None), check_vma=False
    )
```

time: 630 us -> 117 us (0.19)
  waiting for transfers between devices: 306 us -> 0 us
  matrix products: 195 us -> 0 us
  Pallas kernels: 0 us -> 114 us
  local copies, waits for them, and re-layouts: 75.3 us -> 2.31 us
  blocking collectives: 25.3 us -> 0 us
  other arithmetic: 13.6 us -> 0 us
  between operations: 13.9 us -> 0.66 us
    reduce_scatter x2 -> x0, waiting for transfers between devices: 201 us -> none  [on_device(): lax.psum_scatter(flat_terms, 'row', scatter_dimension=0, tiled=True)]
    dot_general x17 -> x0, matrix products: 195 us -> none  [the longest x8 138 us: group_term(): jnp.einsum('rg,gic->ric', placing, product, precision=lax.Precision.HIGHEST)]
    pallas_call x0 -> x1, Pallas kernels: none -> 114 us  [on_device(): pl.pallas_call(make_kernel((slots, bs, rows_n, cols_n)), out_shape=jax.Sh...]
    all_gather x2 -> x0, waiting for transfers between devices: 105 us -> none  [on_device(): lax.all_gather(current.astype(jnp.bfloat16), 'col', axis=0, tiled=True)]
    gather x8 -> x0, local copies, waits for them, and re-layouts: 49.3 us -> none  [group_term(): fetched = jnp.take(gathered, group_cols, axis=0)]
    unnamed x1 -> x0, blocking collectives: 25.3 us -> none
    while x10 -> x0, local copies, waits for them, and re-layouts: 22.9 us -> none  [the longest x2 22.9 us: on_device(): running = lax.fori_loop(0, group_total, add_group, empty)]
  transfers between devices with their start and end apart: 4 -> 0, of which waited for: 4 -> 0; matrix products, arithmetic and copies ran while one was open for 1% -> 0% of each run, Pallas kernels for 0% -> 0%
where the time goes in v2:
time: 117 us
  Pallas kernels  114 us (97%)
  local copies, waits for them, and re-layouts  2.31 us (2%)
    pallas_call x1, Pallas kernels, on_device(): pl.pallas_call(make_kernel((slots, bs, rows_n, cols_n)), out_shape=jax.Sh...  114 us

profile of v2, /device:TPU:0, one launch (start us, length us, event | category | flops | bytes accessed | tf_op | source)
XLA Modules:
  0.0 116.8 jit_solution(17340217024227689300)
XLA Ops:
  0.7 113.8 %shard_map.64 = f32[256,1024]{1,0:T(8,128)} custom-call(s32[1,1,32]{2,1,0:T(1,128)} %rows_s.1, s32[1,1,32]{2,1,0:T(1,128)} %cols_s.1, s32[1,1]{1,0:T(1,128)S(6)} %copy.8.count_s, bf16[1,1,32,256,256]{4,3,2,1,0:T(8,128)(2,1)} %aff.1, f32[256,1024]{1,0:T(8,128)} %labels.1, s32[1,256]{1,0:T(1,128)} %bitcast.1), custom_call_target="tpu_custom_call" | custom-call | tf_op jit(solution)/shard_map/pallas_call | solution.py:358
  114.5 2.3 %copy.9 = f32[256,1024]{1,0:T(8,128)} copy(f32[256,1024]{1,0:T(8,128)} %shard_map.64) | data formatting | bytes 2097152

commit v3 on v2

--- a/solution.py
+++ b/solution.py
@@ -9,20 +9,24 @@
 SWEEPS = 2
 WIDTHS = (256, 256, 256, 256)
 PIECES = 2
-STRIP = 64
+UNROLL = 8
 SPREAD = 0.8
 
 ORDER = (
-    2000, 2010, 0, 3000, 4001, 4000, 4002, 4003, 4011, 4010, 1000, 5001, 5000, 3010, 2020, 5002, 5003, 6000,
-    6001, 7000, 7001, 5011, 4013, 5010, 8001, 4012, 3020, 8000, 2030, 4021, 9000, 5013, 5012, 4020, 10000,
-    10001, 6010, 6011, 7010, 7011, 4023, 4022, 3030, 4030, 11000, 8010, 5021, 9010, 8011, 5023, 5022, 4031,
-    5020, 10010, 10011, 6020, 4032, 4033, 12000, 2040, 6021, 7020, 7021, 5033, 8021, 5030, 11010, 5032, 5031,
-    9020, 8020, 3040, 6030, 4040, 4041, 10020, 10021, 6031, 12010, 2050, 4043, 7030, 8030, 4042, 5040, 5041,
-    7031, 8031, 11020, 3050, 4051, 9030, 4050, 10030, 5042, 5043, 10031, 6040, 12020, 2060, 6041, 7040, 7041,
-    4052, 4053, 8040, 11030, 9040, 5051, 8041, 5050, 4061, 4060, 5052, 5053, 3060, 10040, 10041, 6050, 12030,
-    2070, 6051, 5061, 7050, 7051, 8051, 4062, 4063, 3070, 8050, 4071, 5060, 4070, 11040, 9050, 5063, 5062,
-    10050, 10051, 6060, 4072, 4073, 6061, 7060, 7061, 9060, 5071, 5070, 8060, 8061, 5072, 5073, 6070, 10060,
-    10061, 6071, 7071, 7070, 8070, 12040, 9070, 8071, 11050, 11060, 10070, 10071, 11070, 12060, 12050, 12070,
+    2000, 2010, 0, 3000, 4000, 4001, 4002, 4003, 1000, 3010, 4010, 5000, 4011, 5001, 5002, 5003, 2020, 6000,
+    6001, 7000, 4012, 7002, 7001, 9000, 7003, 4013, 8002, 5011, 8000, 3020, 2030, 5010, 10000, 10002, 8003,
+    4021, 8001, 5012, 5013, 10001, 4020, 10003, 6010, 6011, 11000, 7012, 7010, 7013, 4023, 7011, 4022, 9010,
+    4030, 11001, 4031, 8012, 8010, 3030, 5021, 10010, 10012, 5022, 8013, 5020, 8011, 5023, 10013, 10011,
+    12000, 2040, 6020, 6021, 7020, 7022, 11010, 7021, 4032, 4033, 8020, 7023, 5030, 11011, 5031, 3040, 8022,
+    9020, 4041, 10022, 10020, 8021, 5033, 10023, 5032, 4040, 10021, 8023, 12010, 2050, 6030, 6031, 11020,
+    7030, 7032, 7033, 4043, 7031, 5040, 4042, 8031, 9030, 11021, 3050, 8032, 4050, 5041, 10030, 10032, 8033,
+    8030, 4051, 5043, 5042, 10031, 10033, 12020, 2060, 6040, 6041, 7042, 7040, 4053, 4052, 11030, 7043, 7041,
+    8041, 9040, 3060, 8042, 11031, 5050, 8040, 4061, 8043, 5051, 4060, 10040, 10042, 5052, 5053, 10043, 10041,
+    6050, 12030, 2070, 6051, 7051, 7053, 4062, 5060, 7052, 9050, 7050, 5061, 4063, 11040, 8050, 8053, 8051,
+    8052, 3070, 5063, 5062, 4071, 4070, 10050, 10051, 10052, 10053, 6060, 6061, 4072, 4073, 7060, 7062, 7063,
+    8062, 7061, 8061, 11041, 8060, 9060, 8063, 5071, 5070, 5072, 5073, 10060, 10062, 11050, 6070, 6071, 7070,
+    7072, 8072, 12040, 9070, 10061, 8070, 10070, 10072, 11060, 7073, 10063, 7071, 8073, 11051, 11070, 8071,
+    10073, 10071, 12050, 11061, 12060, 11071, 12070,
 )
 
 PER_NAT = 2048.0 / 0.6931471805599453
@@ -47,14 +51,13 @@
     chunks = len(WIDTHS)
     half = bs // 2
     steps = SWEEPS * chunks
-    per_half = half // STRIP
 
     def kernel(rows_s, cols_s, count_s, aff, labels, marked, out, wv, sums, deg_run, deg_all, inv, mask, prev_s, last_s, *rest):
         xs = rest[:steps]
         pend = rest[steps : 2 * steps]
-        outs = [rest[2 * steps + 14 * q : 2 * steps + 14 * q + 7] for q in range(steps)]
-        ins = [rest[2 * steps + 14 * q + 7 : 2 * steps + 14 * q + 14] for q in range(steps)]
-        (w_sem, xl_sem, z_sem, zr_sem, sib_sem, ag_send, rl_sem, nb_sem, xh_sem, rs_send, dg_recv, dg_send) = rest[16 * steps :]
+        outs = [rest[2 * steps + 26 * q : 2 * steps + 26 * q + 13] for q in range(steps)]
+        ins = [rest[2 * steps + 26 * q + 13 : 2 * steps + 26 * q + 26] for q in range(steps)]
+        (w_sem, xl_sem, z_sem, zr_sem, sib_sem, ag_send, rs_recv, rs_send, dg_recv, dg_send) = rest[28 * steps :]
 
         r, c = lax.axis_index("row"), lax.axis_index("col")
         y, xh = r // 2, r % 2
@@ -67,6 +70,7 @@
         z_to = ((r, col_of(xl, zs[1], core)), (r, col_of(xl, zs[3], core)))
         y_to = ((ys[1] * 2 + xh, c), (ys[3] * 2 + xh, c))
         xh_to = (y * 2 + 1 - xh, c)
+        sides = (1 - xh, xh)
         rows_to = [((r + k) % rows_n, c) for k in range(1, rows_n)]
 
         barrier = pltpu.get_barrier_semaphore()
@@ -88,13 +92,6 @@
                 src_ref=src, dst_ref=dst, send_sem=send, recv_sem=recv, device_id=device, device_id_type=MESH
             )
 
-        def strips(count, body):
-            def step(i, _):
-                body(i)
-                return 0
-
-            lax.fori_loop(0, count, step, 0)
-
         def put(q, ref, recv, device):
             copy(ref, ref, ag_send.at[q], recv, device).start()
 
@@ -103,11 +100,9 @@
 
         def own(q):
             if q < chunks:
-                def cast(i):
-                    at = pl.ds(i * STRIP, STRIP)
+                for h in (0, 1):
+                    at = pl.ds(h * half, half)
                     xs[q][c, at, :] = labels[at, lanes(q)].astype(jnp.bfloat16)
-
-                strips(bs // STRIP, cast)
             block = xs[q].at[c]
             put(q, block, xl_sem.at[q], far_xl)
             put(q, block, z_sem.at[q, 0, 0], z_to[0])
@@ -149,99 +144,72 @@
             wide = pl.ds(0, width(q))
             first = piece * (slots // PIECES)
 
-            def four(i, _):
-                for k in range(4):
-                    s = first + i * 4 + k
+            def several(i, _):
+                for k in range(UNROLL):
+                    s = first + i * UNROLL + k
                     block = xs[q][cols_s[0, 0, s]]
                     sums[s + 1, :, wide] = sums[prev_s[s], :, wide] + jnp.dot(wv[s], block, preferred_element_type=jnp.float32)
                 return 0
 
-            lax.fori_loop(0, slots // PIECES // 4, four, 0)
-
-        def share(q, rho, first):
-            scale = inv[rho, pl.ds(first, STRIP), :]
-            scale = jnp.concatenate([scale] * (width(q) // 128), axis=1)
-            return sums[last_s[rho], pl.ds(first, STRIP), pl.ds(0, width(q))] * scale
-
-        def send_unit(q, unit, recv, device):
-            copy(outs[q][unit], ins[q][unit], rs_send.at[q, unit], recv, device).start()
-
-        def got_unit(q, unit, recv, device):
-            copy(outs[q][unit], ins[q][unit], rs_send.at[q, unit], recv, device).wait_recv()
-
-        def send_far(q, h):
-            def relay(i):
-                side, first = i // per_half, (i % per_half) * STRIP
-                outs[q][h][pl.ds(i * STRIP, STRIP), :] = encode(share(q, ys[2] * 2 + side, h * half + first))
-
-            strips(2 * per_half, relay)
-            send_unit(q, h, rl_sem.at[q, h], y_to[h])
-
-        def send_near(q, d):
-            unit = 3 if d == 0 else 4
-
-            def straight(i):
-                side, first = i // per_half, (i % per_half) * STRIP
-                value = share(q, (ys[1] if d == 0 else ys[3]) * 2 + side, (1 - d) * half + first)
-                outs[q][unit][pl.ds(i * STRIP, STRIP), :] = encode(value)
-
-            strips(2 * per_half, straight)
-            send_unit(q, unit, nb_sem.at[q, d, 1 - d], y_to[d])
+            lax.fori_loop(0, slots // PIECES // UNROLL, several, 0)
+
+        def share(q, rho, h):
+            at = pl.ds(h * half, half)
+            scale = jnp.concatenate([inv[rho, at, :]] * (width(q) // 128), axis=1)
+            return sums[last_s[rho], at, pl.ds(0, width(q))] * scale
+
+        def send_unit(q, unit, device):
+            copy(outs[q][unit], ins[q][unit], rs_send.at[q, unit], rs_recv.at[q, unit], device).start()
+
+        def got_unit(q, unit, device):
+            copy(outs[q][unit], ins[q][unit], rs_send.at[q, unit], rs_recv.at[q, unit], device).wait_recv()
+
+        def next_y(d, o):
+            return (ys[1] if d == 0 else ys[3]) * 2 + sides[o]
+
+        def send_far(q, h, o):
+            unit = 2 * h + o
+            outs[q][unit][...] = encode(share(q, ys[2] * 2 + sides[o], h))
+            send_unit(q, unit, y_to[h])
+
+        def send_near(q, d, o):
+            unit = 4 + 4 * d + 2 * (1 - d) + o
+            outs[q][unit][...] = encode(share(q, next_y(d, o), 1 - d))
+            send_unit(q, unit, y_to[d])
 
         def set_aside(q):
-            for d in (0, 1):
-                def wait_relay(i):
-                    side, first = i // per_half, (i % per_half) * STRIP
-                    value = share(q, (ys[1] if d == 0 else ys[3]) * 2 + side, d * half + first)
-                    pend[q][pl.ds(d * bs + i * STRIP, STRIP), :] = value
-
-                strips(2 * per_half, wait_relay)
-            for side in (0, 1):
-                def stay(i):
-                    pend[q][pl.ds((2 + side) * bs + i * STRIP, STRIP), :] = share(q, y * 2 + side, i * STRIP)
-
-                strips(2 * per_half, stay)
-
-        def relay_on(q, d):
-            unit = 2 if d == 0 else 5
-            got_unit(q, d, rl_sem.at[q, d], y_to[d])
-
-            def joined(i):
-                at = pl.ds(i * STRIP, STRIP)
-                value = pend[q][pl.ds(d * bs + i * STRIP, STRIP), :] + decode(ins[q][d][at, :])
-                outs[q][unit][at, :] = encode(value)
-
-            strips(2 * per_half, joined)
-            send_unit(q, unit, nb_sem.at[q, d, d], y_to[d])
-
-        def in_y(q, side, h, first):
-            at = pl.ds(side * half + first, STRIP)
-            value = pend[q][pl.ds((2 + side) * bs + h * half + first, STRIP), :] + decode(ins[q][2 + h][at, :])
-            return value + decode(ins[q][4 + h][at, :])
-
-        def over_y(q):
+            for o in (0, 1):
+                for d in (0, 1):
+                    pend[q][pl.ds((2 * d + o) * half, half), :] = share(q, next_y(d, o), d)
+                for h in (0, 1):
+                    pend[q][pl.ds((4 + 2 * o + h) * half, half), :] = share(q, y * 2 + sides[o], h)
+
+        def relay_on(q, d, o):
+            unit = 4 + 4 * d + 2 * d + o
+            got_unit(q, 2 * d + o, y_to[d])
+            value = pend[q][pl.ds((2 * d + o) * half, half), :] + decode(ins[q][2 * d + o][...])
+            outs[q][unit][...] = encode(value)
+            send_unit(q, unit, y_to[d])
+
+        def over_y(q, o):
             for h in (0, 1):
                 for d in (0, 1):
-                    got_unit(q, 2 + 2 * d + h, nb_sem.at[q, d, h], y_to[d])
+                    got_unit(q, 4 + 4 * d + 2 * h + o, y_to[d])
             for h in (0, 1):
-                def other(i):
-                    outs[q][6][pl.ds(h * half + i * STRIP, STRIP), :] = encode(in_y(q, 1 - xh, h, i * STRIP))
-
-                strips(per_half, other)
-            send_unit(q, 6, xh_sem.at[q], xh_to)
+                at = pl.ds((4 + 2 * o + h) * half, half)
+                value = pend[q][at, :] + decode(ins[q][4 + 2 * h + o][...]) + decode(ins[q][8 + 2 * h + o][...])
+                if o == 0:
+                    outs[q][12][pl.ds(h * half, half), :] = encode(value)
+                else:
+                    pend[q][at, :] = value
+            if o == 0:
+                send_unit(q, 12, xh_to)
+
+        def finish(q):
+            got_unit(q, 12, xh_to)
             for h in (0, 1):
-                def mine(i):
-                    value = in_y(q, xh, h, i * STRIP)
-                    pend[q][pl.ds((2 + xh) * bs + h * half + i * STRIP, STRIP), :] = value
-
-                strips(per_half, mine)
-
-        def finish(q):
-            got_unit(q, 6, xh_sem.at[q], xh_to)
-
-            def update(i):
-                at = pl.ds(i * STRIP, STRIP)
-                total = pend[q][pl.ds((2 + xh) * bs + i * STRIP, STRIP), :] + decode(ins[q][6][at, :])
+                at = pl.ds(h * half, half)
+                total = pend[q][pl.ds((6 + h) * half, half), :] + decode(ins[q][12][at, :])
                 prior = labels[at, lanes(q)]
                 keep = jnp.concatenate([mask[at, :]] * (width(q) // 128), axis=1)
                 value = jnp.where(keep == 1.0, prior, SPREAD * total + (1.0 - SPREAD) * prior)
@@ -249,8 +217,6 @@
                     xs[q + chunks][c, at, :] = value.astype(jnp.bfloat16)
                 else:
                     out[at, lanes(q)] = value
-
-            strips(2 * per_half, update)
 
         def degrees_out(q):
             live = count_s[0, 0]
@@ -303,9 +269,9 @@
         phases = (degrees_out, degrees_in, own, pair, near, far, prod, send_far, send_near, set_aside, relay_on, over_y, finish)
         for code in ORDER:
             kind, q, more = code // 1000, code // 10 % 100, code % 10
-            if kind in (4, 5):
+            if kind in (4, 5, 7, 8, 10):
                 phases[kind](q, more // 2, more % 2)
-            elif kind in (6, 7, 8, 10):
+            elif kind in (6, 11):
                 phases[kind](q, more)
             else:
                 phases[kind](q)
@@ -313,8 +279,8 @@
         for q in range(steps):
             sent = xs[q].at[pl.ds(0, 15)]
             copy(sent, sent, ag_send.at[q], xl_sem.at[q], sib).wait_send()
-            for unit in range(7):
-                copy(outs[q][unit], ins[q][unit], rs_send.at[q, unit], xh_sem.at[q], xh_to).wait_send()
+            for unit in range(13):
+                copy(outs[q][unit], ins[q][unit], rs_send.at[q, unit], rs_recv.at[q, unit], xh_to).wait_send()
         copy(deg_all.at[pl.ds(0, rows_n - 1)], deg_all.at[pl.ds(0, rows_n - 1)], dg_send, dg_recv.at[0], rows_to[0]).wait_send()
 
     return kernel
@@ -339,17 +305,15 @@
             pltpu.SMEM((rows_n,), jnp.int32),
             *[pltpu.VMEM((cols_n, bs, width), jnp.bfloat16) for width in each],
             *[pltpu.VMEM((4 * bs, width), jnp.float32) for width in each],
-            *[pltpu.VMEM((bs, width), jnp.int16) for width in each for _ in range(14)],
+            *[pltpu.VMEM((rows, width), jnp.int16) for width in each for rows in 2 * ([bs // 2] * 12 + [bs])],
             dma,
             dma((steps,)),
             dma((steps, 2, 2)),
             dma((steps, 2, 2)),
             dma((steps, 10)),
             dma((steps,)),
-            dma((steps, 2)),
-            dma((steps, 2, 2)),
-            dma((steps,)),
-            dma((steps, 7)),
+            dma((steps, 13)),
+            dma((steps, 13)),
             dma((rows_n - 1,)),
             dma,
         ]

time: 117 us -> 111 us (0.949)
  Pallas kernels: 114 us -> 108 us
    pallas_call x1, Pallas kernels: 114 us -> 108 us  [on_device(): pl.pallas_call(make_kernel((slots, bs, rows_n, cols_n)), out_shape=jax.Sh...]
where the time goes in v3:
time: 111 us
  Pallas kernels  108 us (97%)
  local copies, waits for them, and re-layouts  2.31 us (2%)
    pallas_call x1, Pallas kernels, on_device(): pl.pallas_call(make_kernel((slots, bs, rows_n, cols_n)), out_shape=jax.Sh...  108 us
    unnamed x1, local copies, waits for them, and re-layouts  2.31 us

profile of v3, /device:TPU:0, one launch (start us, length us, event | category | flops | bytes accessed | tf_op | source)
XLA Modules:
  0.0 111.1 jit_solution(13365891480353682945)
XLA Ops:
  0.7 108.1 %shard_map.64 = f32[256,1024]{1,0:T(8,128)} custom-call(s32[1,1,32]{2,1,0:T(1,128)} %rows_s.1, s32[1,1,32]{2,1,0:T(1,128)} %cols_s.1, s32[1,1]{1,0:T(1,128)S(6)} %copy.8.count_s, bf16[1,1,32,256,256]{4,3,2,1,0:T(8,128)(2,1)} %aff.1, f32[256,1024]{1,0:T(8,128)} %labels.1, s32[1,256]{1,0:T(1,128)} %bitcast.1), custom_call_target="tpu_custom_call" | custom-call | tf_op jit(solution)/shard_map/pallas_call | solution.py:322
  108.8 2.3 %copy.9 = f32[256,1024]{1,0:T(8,128)} copy(f32[256,1024]{1,0:T(8,128)} %shard_map.64) | data formatting | bytes 2097152

commit v4 on v3

--- a/solution.py
+++ b/solution.py
@@ -13,20 +13,22 @@
 SPREAD = 0.8
 
 ORDER = (
-    2000, 2010, 0, 3000, 4000, 4001, 4002, 4003, 1000, 3010, 4010, 5000, 4011, 5001, 5002, 5003, 2020, 6000,
-    6001, 7000, 4012, 7002, 7001, 9000, 7003, 4013, 8002, 5011, 8000, 3020, 2030, 5010, 10000, 10002, 8003,
-    4021, 8001, 5012, 5013, 10001, 4020, 10003, 6010, 6011, 11000, 7012, 7010, 7013, 4023, 7011, 4022, 9010,
-    4030, 11001, 4031, 8012, 8010, 3030, 5021, 10010, 10012, 5022, 8013, 5020, 8011, 5023, 10013, 10011,
-    12000, 2040, 6020, 6021, 7020, 7022, 11010, 7021, 4032, 4033, 8020, 7023, 5030, 11011, 5031, 3040, 8022,
-    9020, 4041, 10022, 10020, 8021, 5033, 10023, 5032, 4040, 10021, 8023, 12010, 2050, 6030, 6031, 11020,
-    7030, 7032, 7033, 4043, 7031, 5040, 4042, 8031, 9030, 11021, 3050, 8032, 4050, 5041, 10030, 10032, 8033,
-    8030, 4051, 5043, 5042, 10031, 10033, 12020, 2060, 6040, 6041, 7042, 7040, 4053, 4052, 11030, 7043, 7041,
-    8041, 9040, 3060, 8042, 11031, 5050, 8040, 4061, 8043, 5051, 4060, 10040, 10042, 5052, 5053, 10043, 10041,
-    6050, 12030, 2070, 6051, 7051, 7053, 4062, 5060, 7052, 9050, 7050, 5061, 4063, 11040, 8050, 8053, 8051,
-    8052, 3070, 5063, 5062, 4071, 4070, 10050, 10051, 10052, 10053, 6060, 6061, 4072, 4073, 7060, 7062, 7063,
-    8062, 7061, 8061, 11041, 8060, 9060, 8063, 5071, 5070, 5072, 5073, 10060, 10062, 11050, 6070, 6071, 7070,
-    7072, 8072, 12040, 9070, 10061, 8070, 10070, 10072, 11060, 7073, 10063, 7071, 8073, 11051, 11070, 8071,
-    10073, 10071, 12050, 11061, 12060, 11071, 12070,
+    2000, 2010, 0, 3000, 1000, 13011, 4001, 4011, 13010, 4000, 4002, 4003, 4010, 13001, 13000, 5001, 3010,
+    13003, 5000, 5002, 13002, 5003, 2020, 6000, 6001, 7002, 7000, 5011, 4012, 5010, 4013, 13013, 7001, 8002,
+    9000, 8000, 7003, 13012, 3020, 4020, 4021, 10002, 5012, 10000, 5013, 2030, 13020, 8001, 8003, 10001, 6010,
+    10003, 6011, 7010, 7012, 11000, 7011, 7013, 4022, 13021, 4023, 5021, 13023, 5020, 11001, 3030, 8012,
+    13030, 9010, 8010, 13022, 10012, 10010, 5022, 4031, 4030, 5023, 8013, 10013, 8011, 10011, 12000, 2040,
+    6020, 6021, 7020, 7022, 11010, 7023, 4033, 7021, 4032, 5030, 9020, 13031, 4041, 4040, 13040, 8020, 8022,
+    3040, 10020, 11011, 5031, 10022, 5032, 5033, 8021, 13033, 13032, 10023, 10021, 8023, 12010, 2050, 6030,
+    6031, 7030, 7032, 11020, 4043, 4042, 7031, 13043, 13041, 13042, 7033, 9030, 5041, 8031, 8032, 3050, 10032,
+    8030, 5040, 13051, 5042, 10030, 8033, 4051, 4050, 11021, 5043, 10031, 10033, 12020, 2060, 6040, 6041,
+    7040, 4052, 7043, 4053, 13052, 11030, 5050, 8042, 8041, 7041, 13053, 3060, 9040, 5051, 4060, 13050, 7042,
+    5052, 5053, 8040, 4061, 11031, 10043, 10040, 8043, 6050, 12030, 2070, 10041, 10042, 6051, 7050, 5060,
+    13060, 7053, 13063, 4063, 4062, 13062, 5061, 7051, 9050, 7052, 8051, 11040, 3070, 8052, 4071, 10053,
+    13061, 4070, 5062, 5063, 10050, 8053, 8050, 10051, 10052, 6060, 4072, 6061, 7060, 4073, 7062, 9060, 5070,
+    8060, 7063, 13073, 5071, 13070, 13072, 8061, 7061, 13071, 8063, 5072, 5073, 8062, 10062, 10060, 6070,
+    6071, 7072, 7070, 9070, 11050, 8071, 7073, 8070, 8072, 10070, 10072, 11041, 11060, 12040, 7071, 11051,
+    12050, 10063, 10061, 11070, 8073, 10073, 10071, 11061, 12060, 11071, 12070,
 )
 
 PER_NAT = 2048.0 / 0.6931471805599453
@@ -105,22 +107,34 @@
                     xs[q][c, at, :] = labels[at, lanes(q)].astype(jnp.bfloat16)
             block = xs[q].at[c]
             put(q, block, xl_sem.at[q], far_xl)
-            put(q, block, z_sem.at[q, 0, 0], z_to[0])
-            put(q, block, z_sem.at[q, 0, 1], z_to[1])
+            along_z(q, c, 0)
             put(q, block, sib_sem.at[q, 0], sib)
 
         def pair(q):
-            block = xs[q].at[col_of(1 - xl, z, core)]
+            b = col_of(1 - xl, z, core)
+            block = xs[q].at[b]
             got(q, block, xl_sem.at[q], far_xl)
-            put(q, block, z_sem.at[q, 1, 0], z_to[0])
-            put(q, block, z_sem.at[q, 1, 1], z_to[1])
+            along_z(q, b, 1)
             put(q, block, sib_sem.at[q, 1], sib)
+
+        def along_z(q, b, kind):
+            for later in (0, 1):
+                for d in (0, 1):
+                    part = xs[q].at[b, pl.ds(half * (1 - d if later else d), half)]
+                    put(q, part, z_sem.at[q, kind, 2 * d + later], z_to[d])
 
         def near(q, kind, d):
             b = col_of(xl if kind == 0 else 1 - xl, zs[3] if d == 0 else zs[1], core)
-            got(q, xs[q].at[b], z_sem.at[q, kind, d], z_to[d])
-            put(q, xs[q].at[b, pl.ds(half * d, half)], zr_sem.at[q, kind, d], z_to[d])
-            put(q, xs[q].at[b], sib_sem.at[q, 2 + 2 * kind + d], sib)
+            part = xs[q].at[b, pl.ds(half * d, half)]
+            got(q, part, z_sem.at[q, kind, 2 * d], z_to[d])
+            put(q, part, zr_sem.at[q, kind, d], z_to[d])
+            put(q, part, sib_sem.at[q, 2 + 2 * kind + d], sib)
+
+        def near_rest(q, kind, d):
+            b = col_of(xl if kind == 0 else 1 - xl, zs[3] if d == 0 else zs[1], core)
+            part = xs[q].at[b, pl.ds(half * (1 - d), half)]
+            got(q, part, z_sem.at[q, kind, 2 * d + 1], z_to[d])
+            put(q, part, sib_sem.at[q, 10 + 2 * kind + d], sib)
 
         def far(q, kind, d):
             b = col_of(xl if kind == 0 else 1 - xl, zs[2], core)
@@ -133,8 +147,9 @@
                 side = xl if kind == 0 else 1 - xl
                 got(q, xs[q].at[col_of(side, z, 1 - core)], sib_sem.at[q, kind], sib)
                 for d in (0, 1):
-                    block = xs[q].at[col_of(side, zs[3] if d == 0 else zs[1], 1 - core)]
-                    got(q, block, sib_sem.at[q, 2 + 2 * kind + d], sib)
+                    b = col_of(side, zs[3] if d == 0 else zs[1], 1 - core)
+                    got(q, xs[q].at[b, pl.ds(half * d, half)], sib_sem.at[q, 2 + 2 * kind + d], sib)
+                    got(q, xs[q].at[b, pl.ds(half * (1 - d), half)], sib_sem.at[q, 10 + 2 * kind + d], sib)
                     part = xs[q].at[col_of(side, zs[2], 1 - core), pl.ds(half * d, half)]
                     got(q, part, sib_sem.at[q, 6 + 2 * kind + d], sib)
 
@@ -266,10 +281,11 @@
                 inv[rho] = jnp.broadcast_to(turned[:, rho : rho + 1], (bs, 128))
             mask[...] = jnp.broadcast_to(turned[:, rows_n : rows_n + 1], (bs, 128))
 
-        phases = (degrees_out, degrees_in, own, pair, near, far, prod, send_far, send_near, set_aside, relay_on, over_y, finish)
+        phases = (degrees_out, degrees_in, own, pair, near, far, prod, send_far, send_near, set_aside, relay_on, over_y, finish,
+                  near_rest)
         for code in ORDER:
             kind, q, more = code // 1000, code // 10 % 100, code % 10
-            if kind in (4, 5, 7, 8, 10):
+            if kind in (4, 5, 7, 8, 10, 13):
                 phases[kind](q, more // 2, more % 2)
             elif kind in (6, 11):
                 phases[kind](q, more)
@@ -308,9 +324,9 @@
             *[pltpu.VMEM((rows, width), jnp.int16) for width in each for rows in 2 * ([bs // 2] * 12 + [bs])],
             dma,
             dma((steps,)),
+            dma((steps, 2, 4)),
             dma((steps, 2, 2)),
-            dma((steps, 2, 2)),
-            dma((steps, 10)),
+            dma((steps, 14)),
             dma((steps,)),
             dma((steps, 13)),
             dma((steps, 13)),

time: 111 us -> 111 us (level)
  no operation moved by 1% of the time
where the time goes in v4:
time: 111 us
  Pallas kernels  108 us (97%)
  local copies, waits for them, and re-layouts  2.31 us (2%)
    pallas_call x1, Pallas kernels, on_device(): pl.pallas_call(make_kernel((slots, bs, rows_n, cols_n)), out_shape=jax.Sh...  108 us
    unnamed x1, local copies, waits for them, and re-layouts  2.31 us

profile of v4, /device:TPU:0, one launch (start us, length us, event | category | flops | bytes accessed | tf_op | source)
XLA Modules:
  0.0 111.2 jit_solution(1309993581570134447)
XLA Ops:
  0.7 108.2 %shard_map.64 = f32[256,1024]{1,0:T(8,128)} custom-call(s32[1,1,32]{2,1,0:T(1,128)} %rows_s.1, s32[1,1,32]{2,1,0:T(1,128)} %cols_s.1, s32[1,1]{1,0:T(1,128)S(6)} %copy.8.count_s, bf16[1,1,32,256,256]{4,3,2,1,0:T(8,128)(2,1)} %aff.1, f32[256,1024]{1,0:T(8,128)} %labels.1, s32[1,256]{1,0:T(1,128)} %bitcast.1), custom_call_target="tpu_custom_call" | custom-call | tf_op jit(solution)/shard_map/pallas_call | solution.py:338
  108.9 2.3 %copy.9 = f32[256,1024]{1,0:T(8,128)} copy(f32[256,1024]{1,0:T(8,128)} %shard_map.64) | data formatting | bytes 2097152

commit v5 on v3

--- a/solution.py
+++ b/solution.py
@@ -13,20 +13,20 @@
 SPREAD = 0.8
 
 ORDER = (
-    2000, 2010, 0, 3000, 4000, 4001, 4002, 4003, 1000, 3010, 4010, 5000, 4011, 5001, 5002, 5003, 2020, 6000,
-    6001, 7000, 4012, 7002, 7001, 9000, 7003, 4013, 8002, 5011, 8000, 3020, 2030, 5010, 10000, 10002, 8003,
-    4021, 8001, 5012, 5013, 10001, 4020, 10003, 6010, 6011, 11000, 7012, 7010, 7013, 4023, 7011, 4022, 9010,
-    4030, 11001, 4031, 8012, 8010, 3030, 5021, 10010, 10012, 5022, 8013, 5020, 8011, 5023, 10013, 10011,
-    12000, 2040, 6020, 6021, 7020, 7022, 11010, 7021, 4032, 4033, 8020, 7023, 5030, 11011, 5031, 3040, 8022,
-    9020, 4041, 10022, 10020, 8021, 5033, 10023, 5032, 4040, 10021, 8023, 12010, 2050, 6030, 6031, 11020,
-    7030, 7032, 7033, 4043, 7031, 5040, 4042, 8031, 9030, 11021, 3050, 8032, 4050, 5041, 10030, 10032, 8033,
-    8030, 4051, 5043, 5042, 10031, 10033, 12020, 2060, 6040, 6041, 7042, 7040, 4053, 4052, 11030, 7043, 7041,
-    8041, 9040, 3060, 8042, 11031, 5050, 8040, 4061, 8043, 5051, 4060, 10040, 10042, 5052, 5053, 10043, 10041,
-    6050, 12030, 2070, 6051, 7051, 7053, 4062, 5060, 7052, 9050, 7050, 5061, 4063, 11040, 8050, 8053, 8051,
-    8052, 3070, 5063, 5062, 4071, 4070, 10050, 10051, 10052, 10053, 6060, 6061, 4072, 4073, 7060, 7062, 7063,
-    8062, 7061, 8061, 11041, 8060, 9060, 8063, 5071, 5070, 5072, 5073, 10060, 10062, 11050, 6070, 6071, 7070,
-    7072, 8072, 12040, 9070, 10061, 8070, 10070, 10072, 11060, 7073, 10063, 7071, 8073, 11051, 11070, 8071,
-    10073, 10071, 12050, 11061, 12060, 11071, 12070,
+    2000, 0, 2010, 3000, 4001, 4000, 4011, 4002, 4003, 1000, 5001, 5000, 3010, 5011, 5002, 5003, 4010, 2020,
+    6000, 6001, 7000, 7002, 4013, 4012, 5010, 7001, 7003, 3020, 8000, 9000, 2030, 8002, 5013, 10000, 10002,
+    8001, 5012, 10003, 8003, 4021, 10001, 6010, 4020, 6011, 7010, 7012, 11000, 4023, 4022, 7011, 7013, 11001,
+    3030, 8010, 9010, 8012, 5023, 10012, 5021, 10010, 4030, 5022, 4031, 8013, 8011, 5020, 10011, 10013, 12000,
+    2040, 6020, 6021, 7020, 7022, 11010, 4033, 7021, 7023, 5031, 4032, 3040, 8020, 11011, 8022, 4040, 9020,
+    4041, 10022, 10020, 5033, 5030, 5032, 8023, 8021, 10023, 10021, 12010, 2050, 6030, 6031, 7030, 7032,
+    11020, 4043, 5040, 7031, 4042, 7033, 5041, 3050, 9030, 8030, 8032, 4051, 10030, 10032, 11021, 4050, 8031,
+    10031, 8033, 10033, 5043, 5042, 12020, 2060, 6040, 6041, 7043, 7040, 5050, 4053, 4052, 11030, 7042, 8040,
+    3060, 7041, 9040, 8043, 8042, 4061, 11031, 5053, 5051, 5052, 10040, 8041, 4060, 10043, 10042, 6050, 12030,
+    2070, 10041, 6051, 7051, 7053, 4062, 9050, 4063, 7052, 5060, 7050, 11040, 8051, 8053, 3070, 10051, 8050,
+    5061, 10053, 5063, 5062, 8052, 10050, 4070, 4071, 10052, 6060, 6061, 4072, 4073, 7060, 7062, 5071, 5070,
+    9060, 8062, 8061, 8063, 7061, 7063, 5072, 5073, 10060, 8060, 10062, 6070, 6071, 7070, 7072, 11050, 9070,
+    8071, 8070, 7073, 8072, 10072, 10070, 11041, 11060, 12040, 11051, 7071, 12050, 10073, 10063, 10061, 11070,
+    8073, 10071, 11061, 11071, 12060, 12070,
 )
 
 PER_NAT = 2048.0 / 0.6931471805599453

time: 111 us -> 110 us (level)
    pallas_call x1, Pallas kernels: 108 us -> 107 us  [on_device(): pl.pallas_call(make_kernel((slots, bs, rows_n, cols_n)), out_shape=jax.Sh...]
where the time goes in v5:
time: 110 us
  Pallas kernels  107 us (97%)
  local copies, waits for them, and re-layouts  2.31 us (2%)
    pallas_call x1, Pallas kernels, on_device(): pl.pallas_call(make_kernel((slots, bs, rows_n, cols_n)), out_shape=jax.Sh...  107 us
    unnamed x1, local copies, waits for them, and re-layouts  2.31 us

profile of v5, /device:TPU:0, one launch (start us, length us, event | category | flops | bytes accessed | tf_op | source)
XLA Modules:
  0.0 109.6 jit_solution(13556558107105345393)
XLA Ops:
  0.7 106.6 %shard_map.64 = f32[256,1024]{1,0:T(8,128)} custom-call(s32[1,1,32]{2,1,0:T(1,128)} %rows_s.1, s32[1,1,32]{2,1,0:T(1,128)} %cols_s.1, s32[1,1]{1,0:T(1,128)S(6)} %copy.8.count_s, bf16[1,1,32,256,256]{4,3,2,1,0:T(8,128)(2,1)} %aff.1, f32[256,1024]{1,0:T(8,128)} %labels.1, s32[1,256]{1,0:T(1,128)} %bitcast.1), custom_call_target="tpu_custom_call" | custom-call | tf_op jit(solution)/shard_map/pallas_call | solution.py:322
  107.3 2.3 %copy.9 = f32[256,1024]{1,0:T(8,128)} copy(f32[256,1024]{1,0:T(8,128)} %shard_map.64) | data formatting | bytes 2097152
